TPU v7x, 32 devices: a whole 2x2x4 slice. The times are simulated.
32 devices in a mesh: row: 4 (over y, core), col: 8 (over z, x).
Axes of the slice: x: 2, y: 2, z: 4, core: 2. Of those that a mesh axis runs over, the one named last changes fastest.
Arguments:
- left_image: bfloat16 [32, 1024], P('row', 'col'), may hold values from -6 to 6
- right_image: bfloat16 [32, 1024], P('row', 'col'), may hold values from -6 to 6
- first_weight: bfloat16 [32, 9], replicated, may hold values from -2 to 2
- second_weight: bfloat16 [32, 288], replicated, may hold values from -0.375 to 0.375
- third_weight: bfloat16 [32, 288], replicated, may hold values from -0.375 to 0.375
- tile_base: int32 [4, 8], P('row', 'col'), may hold values from 0 to 96, as said below
- tile_width: int32 [4, 8], P('row', 'col'), may hold values from 32 to 128
Outputs:
- aggregated: bfloat16 [32, 1024, 128], P('row', 'col')
Inputs may be any that keep to these rules, and one draw needn't show every extreme that they name: In every tile tile_base + tile_width <= 128; one tile has tile_base 0 and tile_width 128, another has tile_base 128 - 128 // 4 and tile_width 128 // 4.
All inputs are finite; a program needn't handle non-finite values.
Results may differ from a plain program's by a relative error of at most 0.0045.
Values may be sent and summed in bfloat16 or wider, within the bound.
A program may use at most 64 MiB of HBM per device.

v0:
```python
from functools import partial

import jax
import jax.numpy as jnp
from jax import lax
from jax.sharding import PartitionSpec as P

NDISP = 128


PENALTY_SMALL = 0.5
PENALTY_LARGE = 4.0
INVALID_COST = 2.0
BIG_VALUE = 1e30


def padded(x, sides, width):
    for axis, dim in sides:
        size, length = (lax.axis_size(axis), x.shape[dim])
        up = [(i, (i + 1) % size) for i in range(size - 1)]
        down = [(j, i) for i, j in up]
        last = lax.slice_in_dim(x, length - width, length, axis=dim)
        initial = lax.slice_in_dim(x, 0, width, axis=dim)
        before = lax.ppermute(last, axis, up)
        after = lax.ppermute(initial, axis, down)
        x = jnp.concatenate([before, x, after], axis=dim)
    return x


def passed_along(value, axis, steps):
    count = lax.axis_size(axis)
    initial, last = (max(0, -steps), min(count, count - steps))
    return lax.ppermute(value, axis, [(source, source + steps) for source in range(initial, last)])


def conv_valid(source, weight):
    in_chan, ext_rows, ext_cols = source.shape
    out_rows = ext_rows - 2
    out_cols = ext_cols - 2
    pieces = [
        source[:, row_off : row_off + out_rows, col_off : col_off + out_cols]
        for row_off in range(3)
        for col_off in range(3)
    ]
    patches = jnp.stack(pieces, 0).reshape(9 * in_chan, out_rows * out_cols)
    result = jnp.dot(weight, patches, preferred_element_type=jnp.float32)
    return result.reshape(weight.shape[0], out_rows, out_cols)


def tower_valid(source, weights, first_row, first_col, total_rows, total_cols):
    current = source[None]
    for layer_num in range(3):
        result = conv_valid(current, weights[layer_num])
        if layer_num < 2:
            result = jnp.maximum(result, 0.0)
        row_place = first_row + layer_num + 1 + jnp.arange(result.shape[1])
        col_place = first_col + layer_num + 1 + jnp.arange(result.shape[2])
        inside = ((row_place >= 0) & (row_place < total_rows))[:, None] & (
            (col_place >= 0) & (col_place < total_cols)
        )[None, :]
        current = jnp.where(inside[None], result, 0.0).astype(jnp.bfloat16)
    return current


def feature_norm(features):
    return jnp.maximum(jnp.sqrt(jnp.sum(jnp.square(features.astype(jnp.float32)), axis=0)), 1.0)


def correlate(left_feat, right_ext, base_disp, range_width):
    chans, tile_rows, tile_cols = left_feat.shape
    left_norm = feature_norm(left_feat)
    right_norm = feature_norm(right_ext)
    products = jnp.einsum("cyx,cyz->yxz", left_feat, right_ext, preferred_element_type=jnp.float32)
    cosine = products / (left_norm[:, :, None] * right_norm[:, None, :])
    ext_span = 2 * tile_cols
    flattened = cosine.reshape(tile_rows, tile_cols * ext_span)
    flattened = jnp.pad(flattened, ((0, 0), (0, tile_cols)))
    skewed = flattened.reshape(tile_rows, tile_cols, ext_span + 1)
    diagonal_band = skewed[:, :, tile_cols - NDISP + 1 : tile_cols + 1][:, :, ::-1]
    shifts = jnp.arange(NDISP)
    in_range = (shifts >= base_disp) & (shifts < base_disp + range_width)
    return jnp.where(in_range, 1.0 - diagonal_band, INVALID_COST).astype(jnp.bfloat16)


def path_step(previous, column_cost):
    lowest = jnp.min(previous, axis=-1, keepdims=True)
    edge_fill = jnp.full(previous.shape[:-1] + (1,), BIG_VALUE, previous.dtype)
    upper_step = jnp.concatenate([previous[..., 1:], edge_fill], axis=-1)
    lower_step = jnp.concatenate([edge_fill, previous[..., :-1]], axis=-1)
    chosen = jnp.minimum(
        jnp.minimum(previous, jnp.minimum(upper_step, lower_step) + PENALTY_SMALL),
        lowest + PENALTY_LARGE,
    )
    updated = column_cost.astype(jnp.float32) + chosen - lowest
    return (updated, updated)


def make_row_chain(volume, strip_rows):
    col_count = lax.axis_size("col")
    col_place = lax.axis_index("col")
    strips = volume.shape[0] // strip_rows
    turn_count = col_count + strips - 1
    blank_state = jnp.zeros((strip_rows, volume.shape[2]), jnp.float32)

    def advance(summed, state, strip_num, backward):
        final_state, path_costs = lax.scan(
            path_step, state, jnp.swapaxes(volume, 0, 1), reverse=backward
        )
        present = summed
        summed = present + jnp.swapaxes(path_costs, 0, 1)
        return (summed, final_state)

    def no_work(summed, state, strip_num):
        return (summed, blank_state)

    def one_turn(step_num, summed, incoming_fwd, incoming_back):
        fwd_strip = step_num - col_place
        summed, out_fwd = lax.cond(
            (fwd_strip >= 0) & (fwd_strip < strips),
            partial(advance, backward=False),
            no_work,
            summed,
            incoming_fwd,
            jnp.clip(fwd_strip, 0, strips - 1),
        )
        back_strip = step_num - (col_count - 1 - col_place)
        summed, out_back = lax.cond(
            (back_strip >= 0) & (back_strip < strips),
            partial(advance, backward=True),
            no_work,
            summed,
            incoming_back,
            jnp.clip(back_strip, 0, strips - 1),
        )
        bordered = padded(jnp.stack([out_back, out_fwd]), (("col", 0),), 1)
        return (summed, bordered[0], bordered[3])

    return (turn_count, blank_state, one_turn)


def make_column_chain(volume, strip_cols):
    row_count = lax.axis_size("row")
    row_place = lax.axis_index("row")
    strips = volume.shape[1] // strip_cols
    turn_count = row_count + strips - 1
    blank_state = jnp.zeros((strip_cols, volume.shape[2]), jnp.float32)

    def advance(summed, state, strip_num, backward):
        final_state, path_costs = lax.scan(path_step, state, volume, reverse=backward)
        present = summed
        summed = present + path_costs
        return (summed, final_state)

    def no_work(summed, state, strip_num):
        return (summed, blank_state)

    def one_turn(step_num, summed, incoming_down, incoming_up):
        down_strip = step_num - row_place
        summed, out_down = lax.cond(
            (down_strip >= 0) & (down_strip < strips),
            partial(advance, backward=False),
            no_work,
            summed,
            incoming_down,
            jnp.clip(down_strip, 0, strips - 1),
        )
        up_strip = step_num - (row_count - 1 - row_place)
        summed, out_up = lax.cond(
            (up_strip >= 0) & (up_strip < strips),
            partial(advance, backward=True),
            no_work,
            summed,
            incoming_up,
            jnp.clip(up_strip, 0, strips - 1),
        )
        bordered = padded(
            jnp.stack([out_up, out_down]).astype(jnp.bfloat16), (("row", 0),), 1
        ).astype(jnp.float32)
        return (summed, bordered[0], bordered[3])

    return (turn_count, blank_state, one_turn)


def on_device(
    left_image, right_image, first_weight, second_weight, third_weight, tile_base, tile_width
):
    weights = (first_weight, second_weight, third_weight)
    tile_rows, tile_cols = left_image.shape
    margins = padded(jnp.stack([left_image, right_image]), (("row", 1), ("col", 2)), 3)
    total_rows = tile_rows * lax.axis_size("row")
    total_cols = tile_cols * lax.axis_size("col")
    first_row = lax.axis_index("row") * tile_rows - 3
    first_col = lax.axis_index("col") * tile_cols - 3
    left_feat = tower_valid(margins[0], weights, first_row, first_col, total_rows, total_cols)
    neighbour = passed_along(margins[1], "col", 1)
    joined = jnp.concatenate([neighbour[:, :tile_cols], margins[1]], axis=1)
    right_ext = tower_valid(
        joined, weights, first_row, first_col - tile_cols, total_rows, total_cols
    )
    volume = correlate(left_feat, right_ext, tile_base[0, 0], tile_width[0, 0])
    row_turns, row_blank, row_turn = make_row_chain(volume, tile_rows)
    column_turns, column_blank, column_turn = make_column_chain(volume, tile_cols)
    summed = jnp.zeros(volume.shape, jnp.float32)

    def row_loop(step_num, carried):
        return row_turn(step_num, carried[0], carried[1], carried[2])

    def column_loop(step_num, carried):
        return column_turn(step_num, carried[0], carried[1], carried[2])

    summed = lax.fori_loop(0, row_turns, row_loop, (summed, row_blank, row_blank))[0]
    summed = lax.fori_loop(0, column_turns, column_loop, (summed, column_blank, column_blank))[0]
    return (summed * 0.25).astype(jnp.bfloat16)


def solution(mesh):
    placed = (P("row", "col"), P("row", "col"), P(), P(), P(), P("row", "col"), P("row", "col"))
    return jax.shard_map(
        on_device, mesh=mesh, in_specs=placed, out_specs=P("row", "col", None), check_vma=False
    )
```

profile of v0, /device:TPU:0, one launch (start us, length us, event | category | flops | bytes accessed | tf_op | source)
XLA Modules:
  0.0 438.1 jit_solution(17682783420030457512)
XLA Ops:
  0.8 2.4 collective-permute-start.4
  3.2 1.3 collective-permute-start.5
  6.6 1.8 collective-permute-done.5
  9.1 3.4 collective-permute-start.6
  12.5 1.3 collective-permute-start.7
  13.9 4.2 collective-permute-done.7
  20.1 0.9 fusion.6
  22.9 2.2 reshape.361
  26.8 4.5 %collective-permute-start.8 = (bf16[14,134]{1,0:T(8,128)(2,1)S(1)}, bf16[14,134]{1,0:T(8,128)(2,1)S(1)}, u32[]{:S(2)}, u32[]{:S(2)}) collective-permute-start(bf16[14,134]{1,0:T(8,128)(2,1)S(1)} %slice_bitcast_fusion.36), channel_id=1, source_target_pairs={{0,1},{1,2},{2,3},{3,4},{4,5},{5,6},{6,7},{8,9},{9,10},{10,11},{11... | collective-permute-start | bytes 11264 | tf_op jit(solution)/shard_map/ppermute | solution.py:33
  31.6 0.9 collective-permute-done.8
  35.4 0.9 fusion.19
  36.3 0.9 fusion.18
  37.3 0.9 fusion.17
  38.1 1.0 fusion.16
  39.1 1.0 fusion.15
  40.2 0.9 fusion.14
  41.0 1.0 fusion.13
  42.1 1.0 fusion.12
  43.1 4.6 %reshape.364 = bf16[288,2580]{1,0:T(8,128)(2,1)S(1)} reshape(bf16[9,32,10,258]{3,2,1,0:T(8,128)(2,1)} %fusion.12) | data formatting | bytes 2972160 | tf_op jit(solution)/shard_map/reshape | solution.py:45
  51.3 1.3 reshape.368
  53.8 348.5 %while.98 = (s32[]{:T(128)}, f32[8,128,128]{2,0,1:T(8,128)S(1)}, f32[8,128]{1,0:T(8,128)S(1)}, f32[8,128]{1,0:T(8,128)S(1)}, s32[]{:T(128)}, /*index=5*/s32[]{:T...) while((s32[]{:T(128)}, f32[8,128,128]{2,0,1:T(8,128)S(1)}, f32[8,128]{1,0:T(8,128)S(1)}, ...), condition=%wide.region_13.14_spmd, body=%wide.region_2.13_spmd.sunk | while | flops 278545 | bytes 3807795 | solution.py:211
  53.8 35.9 %conditional.8 = (f32[8,128,128]{2,0,1:T(8,128)S(1)}, f32[8,128]{1,0:T(8,128)S(1)}) conditional(s32[]{:T(128)} %convert_element_type.165, f32[8,128,128]{2,0,1:T(8,128)S(1)} %get-tuple-element.1089, (bf16[8,128,128]{2,0,1:T(8,128)(2,1)S(1)}, f32[8,128]{1,0:T(8,128)S(1)}, f32[8,128,128]{2,0,1:T(8,128)S(1)}) %tuple.250), branch_computations={%region_3.3_spmd, %region_4.7_spmd} | conditional | flops 139266 | bytes 1625205 | solution.py:118
  53.9 35.8 %while.94 = (s32[]{:T(128)}, f32[8,128]{1,0:T(8,128)S(1)}, f32[128,8,128]{2,1,0:T(8,128)S(1)}, bf16[128,8,128]{2,1,0:T(8,128)(2,1)S(1)}, s32[]{:T(128)}, /*index=5*/f32[]{:T(128)}) while((s32[]{:T(128)}, f32[8,128]{1,0:T(8,128)S(1)}, f32[128,8,128]{2,1,0:T(8,128)S(1)}, bf16[128,8,128]{2,1,0:T(8,128)(2,1)S(1)}, s32[]{:T(128)}, ...), condition=%wide.region_7.6_spmd, body=%wide.region_5.5_spmd.sunk | while | flops 8194 | bytes 44077 | solution.py:106
  89.8 1.3 collective-permute-start.3
  91.1 4.5 %collective-permute-start.2 = (f32[1,8,128]{2,1,0:T(8,128)S(1)}, f32[1,8,128]{2,1,0:T(8,128)S(1)}, u32[]{:S(2)}, u32[]{:S(2)}) collective-permute-start(f32[1,8,128]{2,1,0:T(8,128)S(1)} %bitcast.290), channel_id=1, source_target_pairs={{0,1},{1,2},{2,3},{3,4},{4,5},{5,6},{6,7},{8,9},{9,10},{10,11},{11... | collective-permute-start | bytes 12296 | tf_op jit(solution)/shard_map/while/body/eval_jaxpr/ppermute | solution.py:24
  95.7 1.3 collective-permute-done.2
  97.0 1.3 collective-permute-start.3
  98.3 40.8 %collective-permute-start.2 = (f32[1,8,128]{2,1,0:T(8,128)S(1)}, f32[1,8,128]{2,1,0:T(8,128)S(1)}, u32[]{:S(2)}, u32[]{:S(2)}) collective-permute-start(f32[1,8,128]{2,1,0:T(8,128)S(1)} %bitcast.290), channel_id=1, source_target_pairs={{0,1},{1,2},{2,3},{3,4},{4,5},{5,6},{6,7},{8,9},{9,10},{10,11},{11... | collective-permute-start | bytes 12296 | tf_op jit(solution)/shard_map/while/body/eval_jaxpr/ppermute | solution.py:24
  139.0 1.3 collective-permute-done.2
  140.3 1.3 collective-permute-start.3
  141.6 5.4 %collective-permute-start.2 = (f32[1,8,128]{2,1,0:T(8,128)S(1)}, f32[1,8,128]{2,1,0:T(8,128)S(1)}, u32[]{:S(2)}, u32[]{:S(2)}) collective-permute-start(f32[1,8,128]{2,1,0:T(8,128)S(1)} %bitcast.290), channel_id=1, source_target_pairs={{0,1},{1,2},{2,3},{3,4},{4,5},{5,6},{6,7},{8,9},{9,10},{10,11},{11... | collective-permute-start | bytes 12296 | tf_op jit(solution)/shard_map/while/body/eval_jaxpr/ppermute | solution.py:24
  147.1 1.3 collective-permute-done.2
  148.4 1.3 collective-permute-start.3
  149.7 41.7 %collective-permute-start.2 = (f32[1,8,128]{2,1,0:T(8,128)S(1)}, f32[1,8,128]{2,1,0:T(8,128)S(1)}, u32[]{:S(2)}, u32[]{:S(2)}) collective-permute-start(f32[1,8,128]{2,1,0:T(8,128)S(1)} %bitcast.290), channel_id=1, source_target_pairs={{0,1},{1,2},{2,3},{3,4},{4,5},{5,6},{6,7},{8,9},{9,10},{10,11},{11... | collective-permute-start | bytes 12296 | tf_op jit(solution)/shard_map/while/body/eval_jaxpr/ppermute | solution.py:24
  191.4 1.3 collective-permute-done.2
  192.7 1.3 collective-permute-start.3
  194.0 5.7 %collective-permute-start.2 = (f32[1,8,128]{2,1,0:T(8,128)S(1)}, f32[1,8,128]{2,1,0:T(8,128)S(1)}, u32[]{:S(2)}, u32[]{:S(2)}) collective-permute-start(f32[1,8,128]{2,1,0:T(8,128)S(1)} %bitcast.290), channel_id=1, source_target_pairs={{0,1},{1,2},{2,3},{3,4},{4,5},{5,6},{6,7},{8,9},{9,10},{10,11},{11... | collective-permute-start | bytes 12296 | tf_op jit(solution)/shard_map/while/body/eval_jaxpr/ppermute | solution.py:24
  199.7 1.3 collective-permute-done.2
  201.0 1.3 collective-permute-start.3
  202.3 39.6 %collective-permute-start.2 = (f32[1,8,128]{2,1,0:T(8,128)S(1)}, f32[1,8,128]{2,1,0:T(8,128)S(1)}, u32[]{:S(2)}, u32[]{:S(2)}) collective-permute-start(f32[1,8,128]{2,1,0:T(8,128)S(1)} %bitcast.290), channel_id=1, source_target_pairs={{0,1},{1,2},{2,3},{3,4},{4,5},{5,6},{6,7},{8,9},{9,10},{10,11},{11... | collective-permute-start | bytes 12296 | tf_op jit(solution)/shard_map/while/body/eval_jaxpr/ppermute | solution.py:24
  241.9 1.3 collective-permute-done.2
  243.2 1.3 collective-permute-start.3
  244.5 113.3 %collective-permute-start.2 = (f32[1,8,128]{2,1,0:T(8,128)S(1)}, f32[1,8,128]{2,1,0:T(8,128)S(1)}, u32[]{:S(2)}, u32[]{:S(2)}) collective-permute-start(f32[1,8,128]{2,1,0:T(8,128)S(1)} %bitcast.290), channel_id=1, source_target_pairs={{0,1},{1,2},{2,3},{3,4},{4,5},{5,6},{6,7},{8,9},{9,10},{10,11},{11... | collective-permute-start | bytes 12296 | tf_op jit(solution)/shard_map/while/body/eval_jaxpr/ppermute | solution.py:24
  357.8 1.3 collective-permute-done.2
  359.1 35.9 %conditional.9 = (f32[8,128,128]{2,0,1:T(8,128)S(1)}, f32[8,128]{1,0:T(8,128)S(1)}) conditional(s32[]{:T(128)} %convert_element_type.164, f32[8,128,128]{2,0,1:T(8,128)S(1)} %get-tuple-element.934, (bf16[8,128,128]{2,0,1:T(8,128)(2,1)S(1)}, f32[8,128]{1,0:T(8,128)S(1)}, f32[8,128,128]{2,0,1:T(8,128)S(1)}) %tuple.251), branch_computations={%region_8.8_spmd, %region_9.12_spmd} | conditional | flops 139267 | bytes 2149525 | solution.py:127
  359.2 35.8 %while.95 = (s32[]{:T(128)}, f32[8,128]{1,0:T(8,128)S(1)}, f32[128,8,128]{2,1,0:T(8,128)S(1)}, bf16[128,8,128]{2,1,0:T(8,128)(2,1)S(1)}, s32[]{:T(128)}, /*index=5*/s32[]{:T(128)}, f32[]{:T(128)}) while((s32[]{:T(128)}, f32[8,128]{1,0:T(8,128)S(1)}, f32[128,8,128]{2,1,0:T(8,128)S(1)}, bf16[128,8,128]{2,1,0:T(8,128)(2,1)S(1)}, s32[]{:T(128)}, ...), condition=%wide.region_12.11_spmd, body=%wide.region_10.10_spmd.sunk | while | flops 8195 | bytes 44097 | solution.py:106
  395.1 1.3 collective-permute-start.3
  396.4 4.5 %collective-permute-start.2 = (f32[1,8,128]{2,1,0:T(8,128)S(1)}, f32[1,8,128]{2,1,0:T(8,128)S(1)}, u32[]{:S(2)}, u32[]{:S(2)}) collective-permute-start(f32[1,8,128]{2,1,0:T(8,128)S(1)} %bitcast.290), channel_id=1, source_target_pairs={{0,1},{1,2},{2,3},{3,4},{4,5},{5,6},{6,7},{8,9},{9,10},{10,11},{11... | collective-permute-start | bytes 12296 | tf_op jit(solution)/shard_map/while/body/eval_jaxpr/ppermute | solution.py:24
  401.0 1.3 collective-permute-done.2
  402.4 35.0 %while.99 = (s32[]{:T(128)}, f32[8,128,128]{2,1,0:T(8,128)S(1)}, f32[128,128]{1,0:T(8,128)S(1)}, f32[128,128]{1,0:T(8,128)S(1)}, s32[]{:T(128)}, /*index=5*/s32[...) while((s32[]{:T(128)}, f32[8,128,128]{2,1,0:T(8,128)S(1)}, f32[128,128]{1,0:T(8,128)S(1)}, ...), condition=%wide.region_25.26_spmd, body=%wide.region_14.25_spmd.sunk | while | flops 720657 | bytes 5900923 | solution.py:212
  402.4 3.0 conditional.10
  402.6 2.7 while.96
  405.5 1.3 collective-permute-start
  406.8 3.0 collective-permute-start.1
  409.9 0.8 collective-permute-done.1
  410.8 1.3 collective-permute-start
  412.1 5.9 %collective-permute-start.1 = (bf16[1,128,128]{2,1,0:T(8,128)(2,1)S(1)}, bf16[1,128,128]{2,1,0:T(8,128)(2,1)S(1)}, u32[]{:S(2)}, u32[]{:S(2)}) collective-permute-start(bf16[1,128,128]{2,1,0:T(8,128)(2,1)S(1)} %get-tuple-element.948), channel_id=1, source_target_pairs={{0,8},{8,16},{16,24},{1,9},{9,17},{17,25},{2,10},{10,18},{18,26},{... | collective-permute-start | bytes 98312 | tf_op jit(solution)/shard_map/while/body/eval_jaxpr/ppermute | solution.py:24
  418.0 0.8 collective-permute-done.1
  419.0 1.3 collective-permute-start
  420.3 7.9 %collective-permute-start.1 = (bf16[1,128,128]{2,1,0:T(8,128)(2,1)S(1)}, bf16[1,128,128]{2,1,0:T(8,128)(2,1)S(1)}, u32[]{:S(2)}, u32[]{:S(2)}) collective-permute-start(bf16[1,128,128]{2,1,0:T(8,128)(2,1)S(1)} %get-tuple-element.948), channel_id=1, source_target_pairs={{0,8},{8,16},{16,24},{1,9},{9,17},{17,25},{2,10},{10,18},{18,26},{... | collective-permute-start | bytes 98312 | tf_op jit(solution)/shard_map/while/body/eval_jaxpr/ppermute | solution.py:24
  429.1 3.1 conditional.11
  429.3 2.7 while.97
  432.2 1.3 collective-permute-start
  433.5 3.0 collective-permute-start.1
  (1294 shorter events, 92.2 us)
Async XLA Ops:
  0.0 25.1 %copy-start = (bf16[32,288]{1,0:T(8,128)(2,1)S(1)}, bf16[32,288]{1,0:T(8,128)(2,1)}, u32[]{:S(2)}) copy-start(bf16[32,288]{1,0:T(8,128)(2,1)} %param.30) | copy-start | bytes 55300
  0.8 5.8 %collective-permute-start.4 = (bf16[2,3,128]{2,1,0:T(4,128)(2,1)S(1)}, bf16[2,3,128]{2,1,0:T(4,128)(2,1)S(1)}, u32[]{:S(2)}, u32[]{:S(2)}) collective-permute-start(bf16[2,3,128]{2,1,0:T(4,128)(2,1)S(1)} %get-tuple-element.729), channel_id=1, source_target_pairs={{0,8},{8,16},{16,24},{1,9},{9,17},{17,25},{2,10},{10,18},{18,26},{... | collective-permute-start | bytes 4616 | tf_op jit(solution)/shard_map/ppermute | solution.py:24
  3.2 5.2 %collective-permute-start.5 = (bf16[2,3,128]{2,1,0:T(4,128)(2,1)S(1)}, bf16[2,3,128]{2,1,0:T(4,128)(2,1)S(1)}, u32[]{:S(2)}, u32[]{:S(2)}) collective-permute-start(bf16[2,3,128]{2,1,0:T(4,128)(2,1)S(1)} %get-tuple-element.730), channel_id=1, source_target_pairs={{8,0},{16,8},{24,16},{9,1},{17,9},{25,17},{10,2},{18,10},{26,18},{... | collective-permute-start | bytes 4616 | tf_op jit(solution)/shard_map/ppermute | solution.py:25
  9.1 4.7 %collective-permute-start.6 = (bf16[2,14,3]{2,1,0:T(8,128)(2,1)S(1)}, bf16[2,14,3]{2,1,0:T(8,128)(2,1)S(1)}, u32[]{:S(2)}, u32[]{:S(2)}) collective-permute-start(bf16[2,14,3]{2,1,0:T(8,128)(2,1)S(1)} %get-tuple-element.727), channel_id=1, source_target_pairs={{0,1},{1,2},{2,3},{3,4},{4,5},{5,6},{6,7},{8,9},{9,10},{10,11},{11... | collective-permute-start | bytes 512 | tf_op jit(solution)/shard_map/ppermute | solution.py:24
  12.5 5.5 %collective-permute-start.7 = (bf16[2,14,3]{2,1,0:T(8,128)(2,1)S(1)}, bf16[2,14,3]{2,1,0:T(8,128)(2,1)S(1)}, u32[]{:S(2)}, u32[]{:S(2)}) collective-permute-start(bf16[2,14,3]{2,1,0:T(8,128)(2,1)S(1)} %get-tuple-element.728), channel_id=1, source_target_pairs={{1,0},{2,1},{3,2},{4,3},{5,4},{6,5},{7,6},{9,8},{10,9},{11,10},{12... | collective-permute-start | bytes 512 | tf_op jit(solution)/shard_map/ppermute | solution.py:25
  22.9 8.4 %copy-start.1 = (bf16[32,288]{1,0:T(8,128)(2,1)S(1)}, bf16[32,288]{1,0:T(8,128)(2,1)}, u32[]{:S(2)}) copy-start(bf16[32,288]{1,0:T(8,128)(2,1)} %param.31) | copy-start | bytes 55300
  25.1 8.7 %copy-start.2 = (bf16[32,9]{0,1:T(8,128)(2,1)S(1)}, bf16[32,9]{0,1:T(8,128)(2,1)}, u32[]{:S(2)}) copy-start(bf16[32,9]{0,1:T(8,128)(2,1)} %param.29) | copy-start | bytes 1732
  26.8 5.7 %collective-permute-start.8 = (bf16[14,134]{1,0:T(8,128)(2,1)S(1)}, bf16[14,134]{1,0:T(8,128)(2,1)S(1)}, u32[]{:S(2)}, u32[]{:S(2)}) collective-permute-start(bf16[14,134]{1,0:T(8,128)(2,1)S(1)} %slice_bitcast_fusion.36), channel_id=1, source_target_pairs={{0,1},{1,2},{2,3},{3,4},{4,5},{5,6},{6,7},{8,9},{9,10},{10,11},{11... | collective-permute-start | bytes 11264 | tf_op jit(solution)/shard_map/ppermute | solution.py:33
  89.8 5.9 %collective-permute-start.3 = (f32[1,8,128]{2,1,0:T(8,128)S(1)}, f32[1,8,128]{2,1,0:T(8,128)S(1)}, u32[]{:S(2)}, u32[]{:S(2)}) collective-permute-start(f32[1,8,128]{2,1,0:T(8,128)S(1)} %bitcast.291), channel_id=1, source_target_pairs={{1,0},{2,1},{3,2},{4,3},{5,4},{6,5},{7,6},{9,8},{10,9},{11,10},{12... | collective-permute-start | bytes 12296 | tf_op jit(solution)/shard_map/while/body/eval_jaxpr/ppermute | solution.py:25
  91.1 5.9 %collective-permute-start.2 = (f32[1,8,128]{2,1,0:T(8,128)S(1)}, f32[1,8,128]{2,1,0:T(8,128)S(1)}, u32[]{:S(2)}, u32[]{:S(2)}) collective-permute-start(f32[1,8,128]{2,1,0:T(8,128)S(1)} %bitcast.290), channel_id=1, source_target_pairs={{0,1},{1,2},{2,3},{3,4},{4,5},{5,6},{6,7},{8,9},{9,10},{10,11},{11... | collective-permute-start | bytes 12296 | tf_op jit(solution)/shard_map/while/body/eval_jaxpr/ppermute | solution.py:24
  97.0 42.1 %collective-permute-start.3 = (f32[1,8,128]{2,1,0:T(8,128)S(1)}, f32[1,8,128]{2,1,0:T(8,128)S(1)}, u32[]{:S(2)}, u32[]{:S(2)}) collective-permute-start(f32[1,8,128]{2,1,0:T(8,128)S(1)} %bitcast.291), channel_id=1, source_target_pairs={{1,0},{2,1},{3,2},{4,3},{5,4},{6,5},{7,6},{9,8},{10,9},{11,10},{12... | collective-permute-start | bytes 12296 | tf_op jit(solution)/shard_map/while/body/eval_jaxpr/ppermute | solution.py:25
  98.3 42.1 %collective-permute-start.2 = (f32[1,8,128]{2,1,0:T(8,128)S(1)}, f32[1,8,128]{2,1,0:T(8,128)S(1)}, u32[]{:S(2)}, u32[]{:S(2)}) collective-permute-start(f32[1,8,128]{2,1,0:T(8,128)S(1)} %bitcast.290), channel_id=1, source_target_pairs={{0,1},{1,2},{2,3},{3,4},{4,5},{5,6},{6,7},{8,9},{9,10},{10,11},{11... | collective-permute-start | bytes 12296 | tf_op jit(solution)/shard_map/while/body/eval_jaxpr/ppermute | solution.py:24
  140.3 6.7 %collective-permute-start.3 = (f32[1,8,128]{2,1,0:T(8,128)S(1)}, f32[1,8,128]{2,1,0:T(8,128)S(1)}, u32[]{:S(2)}, u32[]{:S(2)}) collective-permute-start(f32[1,8,128]{2,1,0:T(8,128)S(1)} %bitcast.291), channel_id=1, source_target_pairs={{1,0},{2,1},{3,2},{4,3},{5,4},{6,5},{7,6},{9,8},{10,9},{11,10},{12... | collective-permute-start | bytes 12296 | tf_op jit(solution)/shard_map/while/body/eval_jaxpr/ppermute | solution.py:25
  141.6 6.8 %collective-permute-start.2 = (f32[1,8,128]{2,1,0:T(8,128)S(1)}, f32[1,8,128]{2,1,0:T(8,128)S(1)}, u32[]{:S(2)}, u32[]{:S(2)}) collective-permute-start(f32[1,8,128]{2,1,0:T(8,128)S(1)} %bitcast.290), channel_id=1, source_target_pairs={{0,1},{1,2},{2,3},{3,4},{4,5},{5,6},{6,7},{8,9},{9,10},{10,11},{11... | collective-permute-start | bytes 12296 | tf_op jit(solution)/shard_map/while/body/eval_jaxpr/ppermute | solution.py:24
  148.4 43.0 %collective-permute-start.3 = (f32[1,8,128]{2,1,0:T(8,128)S(1)}, f32[1,8,128]{2,1,0:T(8,128)S(1)}, u32[]{:S(2)}, u32[]{:S(2)}) collective-permute-start(f32[1,8,128]{2,1,0:T(8,128)S(1)} %bitcast.291), channel_id=1, source_target_pairs={{1,0},{2,1},{3,2},{4,3},{5,4},{6,5},{7,6},{9,8},{10,9},{11,10},{12... | collective-permute-start | bytes 12296 | tf_op jit(solution)/shard_map/while/body/eval_jaxpr/ppermute | solution.py:25
  149.7 43.0 %collective-permute-start.2 = (f32[1,8,128]{2,1,0:T(8,128)S(1)}, f32[1,8,128]{2,1,0:T(8,128)S(1)}, u32[]{:S(2)}, u32[]{:S(2)}) collective-permute-start(f32[1,8,128]{2,1,0:T(8,128)S(1)} %bitcast.290), channel_id=1, source_target_pairs={{0,1},{1,2},{2,3},{3,4},{4,5},{5,6},{6,7},{8,9},{9,10},{10,11},{11... | collective-permute-start | bytes 12296 | tf_op jit(solution)/shard_map/while/body/eval_jaxpr/ppermute | solution.py:24
  192.7 7.0 %collective-permute-start.3 = (f32[1,8,128]{2,1,0:T(8,128)S(1)}, f32[1,8,128]{2,1,0:T(8,128)S(1)}, u32[]{:S(2)}, u32[]{:S(2)}) collective-permute-start(f32[1,8,128]{2,1,0:T(8,128)S(1)} %bitcast.291), channel_id=1, source_target_pairs={{1,0},{2,1},{3,2},{4,3},{5,4},{6,5},{7,6},{9,8},{10,9},{11,10},{12... | collective-permute-start | bytes 12296 | tf_op jit(solution)/shard_map/while/body/eval_jaxpr/ppermute | solution.py:25
  194.0 7.0 %collective-permute-start.2 = (f32[1,8,128]{2,1,0:T(8,128)S(1)}, f32[1,8,128]{2,1,0:T(8,128)S(1)}, u32[]{:S(2)}, u32[]{:S(2)}) collective-permute-start(f32[1,8,128]{2,1,0:T(8,128)S(1)} %bitcast.290), channel_id=1, source_target_pairs={{0,1},{1,2},{2,3},{3,4},{4,5},{5,6},{6,7},{8,9},{9,10},{10,11},{11... | collective-permute-start | bytes 12296 | tf_op jit(solution)/shard_map/while/body/eval_jaxpr/ppermute | solution.py:24
  201.0 40.9 %collective-permute-start.3 = (f32[1,8,128]{2,1,0:T(8,128)S(1)}, f32[1,8,128]{2,1,0:T(8,128)S(1)}, u32[]{:S(2)}, u32[]{:S(2)}) collective-permute-start(f32[1,8,128]{2,1,0:T(8,128)S(1)} %bitcast.291), channel_id=1, source_target_pairs={{1,0},{2,1},{3,2},{4,3},{5,4},{6,5},{7,6},{9,8},{10,9},{11,10},{12... | collective-permute-start | bytes 12296 | tf_op jit(solution)/shard_map/while/body/eval_jaxpr/ppermute | solution.py:25
  202.3 40.9 %collective-permute-start.2 = (f32[1,8,128]{2,1,0:T(8,128)S(1)}, f32[1,8,128]{2,1,0:T(8,128)S(1)}, u32[]{:S(2)}, u32[]{:S(2)}) collective-permute-start(f32[1,8,128]{2,1,0:T(8,128)S(1)} %bitcast.290), channel_id=1, source_target_pairs={{0,1},{1,2},{2,3},{3,4},{4,5},{5,6},{6,7},{8,9},{9,10},{10,11},{11... | collective-permute-start | bytes 12296 | tf_op jit(solution)/shard_map/while/body/eval_jaxpr/ppermute | solution.py:24
  243.2 114.6 %collective-permute-start.3 = (f32[1,8,128]{2,1,0:T(8,128)S(1)}, f32[1,8,128]{2,1,0:T(8,128)S(1)}, u32[]{:S(2)}, u32[]{:S(2)}) collective-permute-start(f32[1,8,128]{2,1,0:T(8,128)S(1)} %bitcast.291), channel_id=1, source_target_pairs={{1,0},{2,1},{3,2},{4,3},{5,4},{6,5},{7,6},{9,8},{10,9},{11,10},{12... | collective-permute-start | bytes 12296 | tf_op jit(solution)/shard_map/while/body/eval_jaxpr/ppermute | solution.py:25
  244.5 114.7 %collective-permute-start.2 = (f32[1,8,128]{2,1,0:T(8,128)S(1)}, f32[1,8,128]{2,1,0:T(8,128)S(1)}, u32[]{:S(2)}, u32[]{:S(2)}) collective-permute-start(f32[1,8,128]{2,1,0:T(8,128)S(1)} %bitcast.290), channel_id=1, source_target_pairs={{0,1},{1,2},{2,3},{3,4},{4,5},{5,6},{6,7},{8,9},{9,10},{10,11},{11... | collective-permute-start | bytes 12296 | tf_op jit(solution)/shard_map/while/body/eval_jaxpr/ppermute | solution.py:24
  395.1 5.9 %collective-permute-start.3 = (f32[1,8,128]{2,1,0:T(8,128)S(1)}, f32[1,8,128]{2,1,0:T(8,128)S(1)}, u32[]{:S(2)}, u32[]{:S(2)}) collective-permute-start(f32[1,8,128]{2,1,0:T(8,128)S(1)} %bitcast.291), channel_id=1, source_target_pairs={{1,0},{2,1},{3,2},{4,3},{5,4},{6,5},{7,6},{9,8},{10,9},{11,10},{12... | collective-permute-start | bytes 12296 | tf_op jit(solution)/shard_map/while/body/eval_jaxpr/ppermute | solution.py:25
  396.4 5.9 %collective-permute-start.2 = (f32[1,8,128]{2,1,0:T(8,128)S(1)}, f32[1,8,128]{2,1,0:T(8,128)S(1)}, u32[]{:S(2)}, u32[]{:S(2)}) collective-permute-start(f32[1,8,128]{2,1,0:T(8,128)S(1)} %bitcast.290), channel_id=1, source_target_pairs={{0,1},{1,2},{2,3},{3,4},{4,5},{5,6},{6,7},{8,9},{9,10},{10,11},{11... | collective-permute-start | bytes 12296 | tf_op jit(solution)/shard_map/while/body/eval_jaxpr/ppermute | solution.py:24
  405.5 4.3 collective-permute-start
  406.8 3.9 collective-permute-start.1
  410.8 7.2 %collective-permute-start = (bf16[1,128,128]{2,1,0:T(8,128)(2,1)S(1)}, bf16[1,128,128]{2,1,0:T(8,128)(2,1)S(1)}, u32[]{:S(2)}, u32[]{:S(2)}) collective-permute-start(bf16[1,128,128]{2,1,0:T(8,128)(2,1)S(1)} %get-tuple-element.947), channel_id=1, source_target_pairs={{8,0},{16,8},{24,16},{9,1},{17,9},{25,17},{10,2},{18,10},{26,18},{... | collective-permute-start | bytes 98312 | tf_op jit(solution)/shard_map/while/body/eval_jaxpr/ppermute | solution.py:25
  412.1 6.7 %collective-permute-start.1 = (bf16[1,128,128]{2,1,0:T(8,128)(2,1)S(1)}, bf16[1,128,128]{2,1,0:T(8,128)(2,1)S(1)}, u32[]{:S(2)}, u32[]{:S(2)}) collective-permute-start(bf16[1,128,128]{2,1,0:T(8,128)(2,1)S(1)} %get-tuple-element.948), channel_id=1, source_target_pairs={{0,8},{8,16},{16,24},{1,9},{9,17},{17,25},{2,10},{10,18},{18,26},{... | collective-permute-start | bytes 98312 | tf_op jit(solution)/shard_map/while/body/eval_jaxpr/ppermute | solution.py:24
  419.0 9.2 %collective-permute-start = (bf16[1,128,128]{2,1,0:T(8,128)(2,1)S(1)}, bf16[1,128,128]{2,1,0:T(8,128)(2,1)S(1)}, u32[]{:S(2)}, u32[]{:S(2)}) collective-permute-start(bf16[1,128,128]{2,1,0:T(8,128)(2,1)S(1)} %get-tuple-element.947), channel_id=1, source_target_pairs={{8,0},{16,8},{24,16},{9,1},{17,9},{25,17},{10,2},{18,10},{26,18},{... | collective-permute-start | bytes 98312 | tf_op jit(solution)/shard_map/while/body/eval_jaxpr/ppermute | solution.py:25
  420.3 8.8 %collective-permute-start.1 = (bf16[1,128,128]{2,1,0:T(8,128)(2,1)S(1)}, bf16[1,128,128]{2,1,0:T(8,128)(2,1)S(1)}, u32[]{:S(2)}, u32[]{:S(2)}) collective-permute-start(bf16[1,128,128]{2,1,0:T(8,128)(2,1)S(1)} %get-tuple-element.948), channel_id=1, source_target_pairs={{0,8},{8,16},{16,24},{1,9},{9,17},{17,25},{2,10},{10,18},{18,26},{... | collective-permute-start | bytes 98312 | tf_op jit(solution)/shard_map/while/body/eval_jaxpr/ppermute | solution.py:24
  432.2 4.3 collective-permute-start
  433.5 3.9 collective-permute-start.1
where the time goes:
time: 447 us; the launch traced here: 438 us
  starting transfers between devices  304 us (68%)
  other arithmetic  57.2 us (13%)
  local copies, waits for them, and re-layouts  46.9 us (10%)
  waiting for transfers between devices  20.6 us (5%)
  loops' own time  4.9 us (1%)
    ppermute x14, starting transfers between devices, padded(): before = lax.ppermute(last, axis, up)  281 us
    reduce_min x274, other arithmetic, path_step(): lowest = jnp.min(previous, axis=-1, keepdims=True)  32.9 us
    slice x272, local copies, waits for them, and re-layouts, path_step(): upper_step = jnp.concatenate([previous[..., 1:], edge_fill], axis=-1)  20.4 us
    dynamic_update_slice x256, other arithmetic, advance(): lax.scan(path_step, state, jnp.swapaxes(volume, 0, 1), reverse=backward)  18.6 us
    ppermute x14, starting transfers between devices, padded(): after = lax.ppermute(initial, axis, down)  18 us
    ppermute x14, waiting for transfers between devices, padded(): before = lax.ppermute(last, axis, up)  13.7 us
    unnamed x40, local copies, waits for them, and re-layouts  10.9 us
  transfers between devices with their start and end apart: 29, of which 15 were waited for; matrix products, arithmetic and copies ran while one was open for 0% of the time, Pallas kernels for 0%

commit v1 on v0

v1 whole, which is shorter than its diff:
```python
from functools import partial

import jax
import jax.numpy as jnp
from jax import lax
from jax.experimental import pallas as pl
from jax.experimental.pallas import tpu as pltpu
from jax.sharding import PartitionSpec as P

NDISP = 128
MESH = pl.DeviceIdType.MESH


PENALTY_SMALL = 0.5
PENALTY_LARGE = 4.0
INVALID_COST = 2.0
BIG_VALUE = 1e30


def padded(x, sides, width):
    for axis, dim in sides:
        size, length = (lax.axis_size(axis), x.shape[dim])
        up = [(i, (i + 1) % size) for i in range(size - 1)]
        down = [(j, i) for i, j in up]
        last = lax.slice_in_dim(x, length - width, length, axis=dim)
        initial = lax.slice_in_dim(x, 0, width, axis=dim)
        before = lax.ppermute(last, axis, up)
        after = lax.ppermute(initial, axis, down)
        x = jnp.concatenate([before, x, after], axis=dim)
    return x


def passed_along(value, axis, steps):
    count = lax.axis_size(axis)
    initial, last = (max(0, -steps), min(count, count - steps))
    return lax.ppermute(value, axis, [(source, source + steps) for source in range(initial, last)])


def conv_valid(source, weight):
    in_chan, ext_rows, ext_cols = source.shape
    out_rows = ext_rows - 2
    out_cols = ext_cols - 2
    pieces = [
        source[:, row_off : row_off + out_rows, col_off : col_off + out_cols]
        for row_off in range(3)
        for col_off in range(3)
    ]
    patches = jnp.stack(pieces, 0).reshape(9 * in_chan, out_rows * out_cols)
    result = jnp.dot(weight, patches, preferred_element_type=jnp.float32)
    return result.reshape(weight.shape[0], out_rows, out_cols)


def tower_valid(source, weights, first_row, first_col, total_rows, total_cols):
    current = source[None]
    for layer_num in range(3):
        result = conv_valid(current, weights[layer_num])
        if layer_num < 2:
            result = jnp.maximum(result, 0.0)
        row_place = first_row + layer_num + 1 + jnp.arange(result.shape[1])
        col_place = first_col + layer_num + 1 + jnp.arange(result.shape[2])
        inside = ((row_place >= 0) & (row_place < total_rows))[:, None] & (
            (col_place >= 0) & (col_place < total_cols)
        )[None, :]
        current = jnp.where(inside[None], result, 0.0).astype(jnp.bfloat16)
    return current


def feature_norm(features):
    return jnp.maximum(jnp.sqrt(jnp.sum(jnp.square(features.astype(jnp.float32)), axis=0)), 1.0)


def correlate(left_feat, right_ext, base_disp, range_width):
    chans, tile_rows, tile_cols = left_feat.shape
    left_norm = feature_norm(left_feat)
    right_norm = feature_norm(right_ext)
    products = jnp.einsum("cyx,cyz->yxz", left_feat, right_ext, preferred_element_type=jnp.float32)
    cosine = products / (left_norm[:, :, None] * right_norm[:, None, :])
    ext_span = 2 * tile_cols
    flattened = cosine.reshape(tile_rows, tile_cols * ext_span)
    flattened = jnp.pad(flattened, ((0, 0), (0, tile_cols)))
    skewed = flattened.reshape(tile_rows, tile_cols, ext_span + 1)
    diagonal_band = skewed[:, :, tile_cols - NDISP + 1 : tile_cols + 1][:, :, ::-1]
    shifts = jnp.arange(NDISP)
    in_range = (shifts >= base_disp) & (shifts < base_disp + range_width)
    return jnp.where(in_range, 1.0 - diagonal_band, INVALID_COST).astype(jnp.bfloat16)


def mesh_barrier(col, cols, row, rows):
    barrier = pltpu.get_barrier_semaphore()
    count = jnp.int32(0)
    for axis, place, size in (("col", col, cols), ("row", row, rows)):
        for step in (-1, 1):
            there = (place + step >= 0) & (place + step < size)

            @pl.when(there)
            def _():
                pl.semaphore_signal(
                    barrier, inc=1, device_id={axis: place + step}, device_id_type=MESH
                )

            count = count + there.astype(jnp.int32)
    return barrier, count


def path_kernel(
    tile_rows,
    tile_cols,
    volume_ref,
    out_ref,
    cost,
    acc,
    h_send,
    h_recv,
    v_send,
    v_recv,
    h_send_sem,
    h_recv_sem,
    v_send_sem,
    v_recv_sem,
):
    cols, rows = lax.axis_size("col"), lax.axis_size("row")
    col, row = lax.axis_index("col"), lax.axis_index("row")
    barrier, count = mesh_barrier(col, cols, row, rows)
    cost[...] = volume_ref[...].astype(jnp.float32)
    acc[...] = jnp.zeros_like(acc)
    pl.semaphore_wait(barrier, count)

    def edges(shape):
        lane = lax.broadcasted_iota(jnp.int32, shape, 1)
        low_edge = jnp.where(lane == 0, BIG_VALUE, PENALTY_SMALL)
        high_edge = jnp.where(lane == NDISP - 1, BIG_VALUE, PENALTY_SMALL)
        return low_edge, high_edge

    def near(state, low_edge, high_edge):
        return jnp.minimum(
            state,
            jnp.minimum(
                pltpu.roll(state, 1, 1) + low_edge, pltpu.roll(state, NDISP - 1, 1) + high_edge
            ),
        )

    def run(axis, place, size, backward, send, recv, send_sem, recv_sem, sweep):
        way = backward.astype(jnp.int32)
        step = 1 - 2 * way
        has_source = (place - step >= 0) & (place - step < size)
        has_target = (place + step >= 0) & (place + step < size)
        copy = pltpu.make_async_remote_copy(
            src_ref=send.at[way],
            dst_ref=recv.at[way],
            send_sem=send_sem.at[way],
            recv_sem=recv_sem.at[way],
            device_id={axis: place + step},
            device_id_type=MESH,
        )

        @pl.when(has_source)
        def _():
            copy.wait_recv()

        @pl.when(jnp.logical_not(has_source))
        def _():
            recv[way] = jnp.zeros(recv.shape[1:], jnp.float32)

        send[way] = sweep(recv[way], backward)

        @pl.when(has_target)
        def _():
            copy.start()

        return copy, has_target

    def row_sweep(state, backward):
        low_edge, high_edge = edges(state.shape)

        def body(index, state):
            place = jnp.where(backward, tile_cols - 1 - index, index)
            where = pl.ds(place, tile_rows, stride=tile_cols)
            here = cost[where, :]
            lowest = jnp.min(state, axis=1, keepdims=True)
            updated = jnp.minimum(
                near(state, low_edge, high_edge) + here, lowest + (here + PENALTY_LARGE)
            )
            acc[where, :] = acc[where, :] + (updated - lowest)
            return updated

        state = lax.fori_loop(0, tile_cols, body, state, unroll=4)
        return state - jnp.min(state, axis=1, keepdims=True)

    def column_sweep(state, backward):
        low_edge, high_edge = edges((8, NDISP))

        def body(index, carried):
            place = jnp.where(backward, tile_rows - 1 - index, index)
            new = []
            for piece, state in enumerate(carried):
                where = pl.ds(pl.multiple_of(place * tile_cols + piece * 8, 8), 8)
                lowest = jnp.min(state, axis=1, keepdims=True)
                updated = (
                    jnp.minimum(near(state, low_edge, high_edge), lowest + PENALTY_LARGE)
                    - lowest
                    + cost[where, :]
                )
                acc[where, :] = acc[where, :] + updated
                new.append(updated)
            return tuple(new)

        pieces = tuple(state[i * 8 : i * 8 + 8] for i in range(tile_cols // 8))
        return jnp.concatenate(lax.fori_loop(0, tile_rows, body, pieces), axis=0)

    def horizontal(turn):
        right_half = col > cols - 1 - col
        backward = right_half if turn == 0 else jnp.logical_not(right_half)
        return run(
            "col", col, cols, backward, h_send, h_recv, h_send_sem, h_recv_sem, row_sweep
        )

    def vertical():
        def one(turn, carried):
            lower_half = row > rows - 1 - row
            backward = lower_half != (turn == 1)
            copy, sent = run(
                "row", row, rows, backward, v_send, v_recv, v_send_sem, v_recv_sem, column_sweep
            )

            @pl.when(sent)
            def _():
                copy.wait_send()

            return carried

        lax.fori_loop(0, 2, one, 0)

    late = 2 * jnp.minimum(col, cols - 1 - col) >= cols // 2

    @pl.when(late)
    def _():
        vertical()

    first, first_sent = horizontal(0)

    @pl.when(jnp.logical_not(late))
    def _():
        vertical()

    second, second_sent = horizontal(1)
    out_ref[...] = (acc[...] * 0.25).astype(jnp.bfloat16)

    @pl.when(first_sent)
    def _():
        first.wait_send()

    @pl.when(second_sent)
    def _():
        second.wait_send()


def aggregate(volume):
    tile_rows, tile_cols, disps = volume.shape
    count = tile_rows * tile_cols
    out = pl.pallas_call(
        partial(path_kernel, tile_rows, tile_cols),
        out_shape=jax.ShapeDtypeStruct((count, disps), jnp.bfloat16),
        in_specs=[pl.BlockSpec(memory_space=pltpu.VMEM)],
        out_specs=pl.BlockSpec(memory_space=pltpu.VMEM),
        scratch_shapes=[
            pltpu.VMEM((count, disps), jnp.float32),
            pltpu.VMEM((count, disps), jnp.float32),
            pltpu.VMEM((2, tile_rows, disps), jnp.float32),
            pltpu.VMEM((2, tile_rows, disps), jnp.float32),
            pltpu.VMEM((2, tile_cols, disps), jnp.float32),
            pltpu.VMEM((2, tile_cols, disps), jnp.float32),
            pltpu.SemaphoreType.DMA((2,)),
            pltpu.SemaphoreType.DMA((2,)),
            pltpu.SemaphoreType.DMA((2,)),
            pltpu.SemaphoreType.DMA((2,)),
        ],
        compiler_params=pltpu.CompilerParams(collective_id=0, has_side_effects=True),
        name="paths",
    )(volume.reshape(count, disps))
    return out.reshape(tile_rows, tile_cols, disps)


def on_device(
    left_image, right_image, first_weight, second_weight, third_weight, tile_base, tile_width
):
    weights = (first_weight, second_weight, third_weight)
    tile_rows, tile_cols = left_image.shape
    margins = padded(jnp.stack([left_image, right_image]), (("row", 1), ("col", 2)), 3)
    total_rows = tile_rows * lax.axis_size("row")
    total_cols = tile_cols * lax.axis_size("col")
    first_row = lax.axis_index("row") * tile_rows - 3
    first_col = lax.axis_index("col") * tile_cols - 3
    left_feat = tower_valid(margins[0], weights, first_row, first_col, total_rows, total_cols)
    neighbour = passed_along(margins[1], "col", 1)
    joined = jnp.concatenate([neighbour[:, :tile_cols], margins[1]], axis=1)
    right_ext = tower_valid(
        joined, weights, first_row, first_col - tile_cols, total_rows, total_cols
    )
    volume = correlate(left_feat, right_ext, tile_base[0, 0], tile_width[0, 0])
    return aggregate(volume)


def solution(mesh):
    placed = (P("row", "col"), P("row", "col"), P(), P(), P(), P("row", "col"), P("row", "col"))
    return jax.shard_map(
        on_device, mesh=mesh, in_specs=placed, out_specs=P("row", "col", None), check_vma=False
    )
```

time: 447 us -> 160 us (0.36); the launches traced: 438 us -> 160 us
  starting transfers between devices: 304 us -> 15.9 us
  Pallas kernels: 0 us -> 106 us
  other arithmetic: 57.2 us -> 3.93 us
  waiting for transfers between devices: 20.6 us -> 1.31 us
  local copies, waits for them, and re-layouts: 46.9 us -> 27.7 us
  loops' own time: 4.9 us -> 0 us
    ppermute x14 -> x2, starting transfers between devices: 281 us -> 8.53 us  [padded(): before = lax.ppermute(last, axis, up)]
    pallas_call x0 -> x1, Pallas kernels: none -> 106 us  [aggregate(): pl.pallas_call(partial(path_kernel, tile_rows, tile_cols), out_shape=jax....]
    reduce_min x274 -> x0, other arithmetic: 32.9 us -> none  [path_step(): lowest = jnp.min(previous, axis=-1, keepdims=True)]
    slice x272 -> x0, local copies, waits for them, and re-layouts: 20.4 us -> none  [path_step(): upper_step = jnp.concatenate([previous[..., 1:], edge_fill], axis=-1)]
    dynamic_update_slice x256 -> x0, other arithmetic: 18.6 us -> none  [advance(): lax.scan(path_step, state, jnp.swapaxes(volume, 0, 1), reverse=backward)]
    ppermute x14 -> x2, starting transfers between devices: 18 us -> 2.57 us  [padded(): after = lax.ppermute(initial, axis, down)]
    ppermute x14 -> x2, waiting for transfers between devices: 13.7 us -> 1.3 us  [padded(): before = lax.ppermute(last, axis, up)]
    ppermute x14 -> x2, waiting for transfers between devices: 6.02 us -> 0.01 us  [padded(): after = lax.ppermute(initial, axis, down)]
  transfers between devices with their start and end apart: 29 -> 5, of which waited for: 15 -> 1; matrix products, arithmetic and copies ran while one was open for 0% -> 5% of each run, Pallas kernels for 0% -> 0%
where the time goes in v1:
time: 160 us
  Pallas kernels  106 us (66%)
  local copies, waits for them, and re-layouts  27.7 us (17%)
  starting transfers between devices  15.9 us (10%)
  other arithmetic  3.93 us (2%)
  matrix products  2.79 us (2%)
  between operations  1.95 us (1%)
    pallas_call x1, Pallas kernels, aggregate(): pl.pallas_call(partial(path_kernel, tile_rows, tile_cols), out_shape=jax....  106 us
    unnamed x41, local copies, waits for them, and re-layouts  12.6 us
    ppermute x2, starting transfers between devices, padded(): before = lax.ppermute(last, axis, up)  8.53 us
    reshape x2, local copies, waits for them, and re-layouts, conv_valid(): patches = jnp.stack(pieces, 0).reshape(9 * in_chan, out_rows * out_cols)  6.98 us
    ppermute x1, starting transfers between devices, passed_along(): lax.ppermute(value, axis, [(source, source + steps) for source in range(i...  4.82 us
    another operation x24, local copies, waits for them, and re-layouts, conv_valid(): patches = jnp.stack(pieces, 0).reshape(9 * in_chan, out_rows * out_cols)  3.71 us
  transfers between devices with their start and end apart: 5, of which 1 were waited for; matrix products, arithmetic and copies ran while one was open for 5% of the time, Pallas kernels for 0%

profile of v1, /device:TPU:0, one launch (start us, length us, event | category | flops | bytes accessed | tf_op | source)
XLA Modules:
  0.0 159.9 jit_solution(1838700399894231508)
XLA Ops:
  0.0 0.8 fusion.45
  0.8 1.3 collective-permute-start.1
  2.1 3.0 %collective-permute-start = (bf16[2,3,128]{2,1,0:T(4,128)(2,1)S(1)}, bf16[2,3,128]{2,1,0:T(4,128)(2,1)S(1)}, u32[]{:S(2)}, u32[]{:S(2)}) collective-permute-start(bf16[2,3,128]{2,1,0:T(4,128)(2,1)S(1)} %get-tuple-element.25), channel_id=1, source_target_pairs={{0,8},{8,16},{16,24},{1,9},{9,17},{17,25},{2,10},{10,18},{18,26},{... | collective-permute-start | bytes 4616 | tf_op jit(solution)/shard_map/ppermute | solution.py:27
  7.2 0.7 pad_maximum_fusion.1
  8.0 1.3 collective-permute-start.3
  9.3 5.5 %collective-permute-start.2 = (bf16[2,14,3]{2,1,0:T(8,128)(2,1)S(1)}, bf16[2,14,3]{2,1,0:T(8,128)(2,1)S(1)}, u32[]{:S(2)}, u32[]{:S(2)}) collective-permute-start(bf16[2,14,3]{2,1,0:T(8,128)(2,1)S(1)} %get-tuple-element.23), channel_id=1, source_target_pairs={{0,1},{1,2},{2,3},{3,4},{4,5},{5,6},{6,7},{8,9},{9,10},{10,11},{11... | collective-permute-start | bytes 512 | tf_op jit(solution)/shard_map/ppermute | solution.py:27
  14.8 1.3 collective-permute-done.2
  16.1 0.8 pad_maximum_fusion
  17.0 4.8 %collective-permute-start.4 = (bf16[14,134]{1,0:T(8,128)(2,1)S(1)}, bf16[14,134]{1,0:T(8,128)(2,1)S(1)}, u32[]{:S(2)}, u32[]{:S(2)}) collective-permute-start(bf16[14,134]{1,0:T(8,128)(2,1)S(1)} %slice_bitcast_fusion.36), channel_id=1, source_target_pairs={{0,1},{1,2},{2,3},{3,4},{4,5},{5,6},{6,7},{8,9},{9,10},{10,11},{11... | collective-permute-start | bytes 11264 | tf_op jit(solution)/shard_map/ppermute | solution.py:36
  22.8 0.1 stack.201
  22.9 0.9 fusion.2
  23.8 0.5 max.85
  24.5 0.1 fusion.25
  24.6 0.1 fusion.24
  24.9 0.2 fusion.22
  25.1 0.2 fusion.21
  25.3 0.2 fusion.19
  25.5 0.2 fusion.18
  25.8 2.4 %reshape.337 = bf16[288,1300]{1,0:T(8,128)(2,1)S(1)} reshape(bf16[9,32,10,130]{3,2,1,0:T(8,128)(2,1)S(1)} %fusion.18) | data formatting | bytes 1497600 | tf_op jit(solution)/shard_map/reshape | solution.py:48
  28.2 0.3 fusion.3
  28.4 0.5 max.90
  29.2 0.1 constant_dynamic-update-slice_fusion.4
  29.4 0.1 constant_dynamic-update-slice_fusion.3
  29.5 0.1 constant_dynamic-update-slice_fusion.1
  29.7 0.1 constant_dynamic-update-slice_fusion
  29.8 0.2 multiply_reduce_fusion.1
  30.2 0.1 stack.222
  30.3 0.1 stack.223
  30.4 0.1 stack.224
  30.6 0.1 stack.225
  30.7 0.1 stack.226
  30.8 0.1 stack.227
  30.9 0.1 stack.228
  31.0 0.1 stack.229
  31.1 0.1 stack.230
  31.3 0.2 stack.231
  31.5 0.3 fusion
  31.7 0.4 max.95
  32.2 0.8 fusion.16
  33.0 1.0 fusion.15
  34.0 1.0 fusion.14
  34.9 0.9 fusion.13
  35.8 1.0 fusion.12
  36.8 1.0 fusion.11
  37.8 0.9 fusion.10
  38.7 1.0 fusion.9
  39.7 1.0 fusion.8
  40.7 4.6 %reshape.340 = bf16[288,2580]{1,0:T(8,128)(2,1)S(1)} reshape(bf16[9,32,10,258]{3,2,1,0:T(8,128)(2,1)} %fusion.8) | data formatting | bytes 2972160 | tf_op jit(solution)/shard_map/reshape | solution.py:48
  45.3 0.4 fusion.1
  45.7 0.3 max.100
  46.4 0.1 fusion.34
  46.6 0.1 fusion.33
  46.8 0.1 fusion.31
  46.9 0.1 fusion.30
  47.1 0.3 copy.15
  47.4 0.4 multiply_reduce_fusion
  47.8 0.4 fusion.4
  48.2 0.6 copy.16
  48.9 1.3 reshape.344
  50.2 0.2 slice.315
  50.4 0.7 rev.3
  51.1 0.8 select_convert_fusion.2
  51.9 106.4 %paths.1 = bf16[1024,128]{1,0:T(8,128)(2,1)} custom-call(bf16[1024,128]{1,0:T(8,128)(2,1)} %bitcast.228), custom_call_target="tpu_custom_call" | custom-call | tf_op jit(solution)/shard_map/paths/pallas_call | solution.py:260
  158.3 1.7 %copy.62 = bf16[8,128,128]{2,1,0:T(8,128)(2,1)} copy(bf16[8,128,128]{2,1,0:T(8,128)(2,1)} %bitcast.227) | data formatting | bytes 524288
  (68 shorter events, 3.1 us)
Async XLA Ops:
  0.0 28.2 %copy-start = (bf16[32,288]{1,0:T(8,128)(2,1)S(1)}, bf16[32,288]{1,0:T(8,128)(2,1)}, u32[]{:S(2)}) copy-start(bf16[32,288]{1,0:T(8,128)(2,1)} %param.10) | copy-start | bytes 55300
  0.8 6.4 %collective-permute-start.1 = (bf16[2,3,128]{2,1,0:T(4,128)(2,1)S(1)}, bf16[2,3,128]{2,1,0:T(4,128)(2,1)S(1)}, u32[]{:S(2)}, u32[]{:S(2)}) collective-permute-start(bf16[2,3,128]{2,1,0:T(4,128)(2,1)S(1)} %get-tuple-element.26), channel_id=1, source_target_pairs={{8,0},{16,8},{24,16},{9,1},{17,9},{25,17},{10,2},{18,10},{26,18},{... | collective-permute-start | bytes 4616 | tf_op jit(solution)/shard_map/ppermute | solution.py:28
  2.1 5.1 %collective-permute-start = (bf16[2,3,128]{2,1,0:T(4,128)(2,1)S(1)}, bf16[2,3,128]{2,1,0:T(4,128)(2,1)S(1)}, u32[]{:S(2)}, u32[]{:S(2)}) collective-permute-start(bf16[2,3,128]{2,1,0:T(4,128)(2,1)S(1)} %get-tuple-element.25), channel_id=1, source_target_pairs={{0,8},{8,16},{16,24},{1,9},{9,17},{17,25},{2,10},{10,18},{18,26},{... | collective-permute-start | bytes 4616 | tf_op jit(solution)/shard_map/ppermute | solution.py:27
  8.0 6.8 %collective-permute-start.3 = (bf16[2,14,3]{2,1,0:T(8,128)(2,1)S(1)}, bf16[2,14,3]{2,1,0:T(8,128)(2,1)S(1)}, u32[]{:S(2)}, u32[]{:S(2)}) collective-permute-start(bf16[2,14,3]{2,1,0:T(8,128)(2,1)S(1)} %get-tuple-element.24), channel_id=1, source_target_pairs={{1,0},{2,1},{3,2},{4,3},{5,4},{6,5},{7,6},{9,8},{10,9},{11,10},{12... | collective-permute-start | bytes 512 | tf_op jit(solution)/shard_map/ppermute | solution.py:28
  9.3 6.9 %collective-permute-start.2 = (bf16[2,14,3]{2,1,0:T(8,128)(2,1)S(1)}, bf16[2,14,3]{2,1,0:T(8,128)(2,1)S(1)}, u32[]{:S(2)}, u32[]{:S(2)}) collective-permute-start(bf16[2,14,3]{2,1,0:T(8,128)(2,1)S(1)} %get-tuple-element.23), channel_id=1, source_target_pairs={{0,1},{1,2},{2,3},{3,4},{4,5},{5,6},{6,7},{8,9},{9,10},{10,11},{11... | collective-permute-start | bytes 512 | tf_op jit(solution)/shard_map/ppermute | solution.py:27
  17.0 13.1 %collective-permute-start.4 = (bf16[14,134]{1,0:T(8,128)(2,1)S(1)}, bf16[14,134]{1,0:T(8,128)(2,1)S(1)}, u32[]{:S(2)}, u32[]{:S(2)}) collective-permute-start(bf16[14,134]{1,0:T(8,128)(2,1)S(1)} %slice_bitcast_fusion.36), channel_id=1, source_target_pairs={{0,1},{1,2},{2,3},{3,4},{4,5},{5,6},{6,7},{8,9},{9,10},{10,11},{11... | collective-permute-start | bytes 11264 | tf_op jit(solution)/shard_map/ppermute | solution.py:36
  25.7 4.1 %copy-start.1 = (bf16[32,288]{1,0:T(8,128)(2,1)S(1)}, bf16[32,288]{1,0:T(8,128)(2,1)}, u32[]{:S(2)}) copy-start(bf16[32,288]{1,0:T(8,128)(2,1)} %param.11) | copy-start | bytes 55300
  28.2 3.3 %copy-start.2 = (bf16[32,9]{0,1:T(8,128)(2,1)S(1)}, bf16[32,9]{0,1:T(8,128)(2,1)}, u32[]{:S(2)}) copy-start(bf16[32,9]{0,1:T(8,128)(2,1)} %param.9) | copy-start | bytes 1732

commit v2 on v1

--- a/solution.py
+++ b/solution.py
@@ -102,13 +102,20 @@
     return barrier, count
 
 
+SUBS = 8
+LEADS = NDISP // SUBS
+
+
 def path_kernel(
     tile_rows,
     tile_cols,
     volume_ref,
     out_ref,
-    cost,
-    acc,
+    v_cost,
+    h_cost,
+    h_path,
+    v_path,
+    total,
     h_send,
     h_recv,
     v_send,
@@ -121,23 +128,65 @@
     cols, rows = lax.axis_size("col"), lax.axis_size("row")
     col, row = lax.axis_index("col"), lax.axis_index("row")
     barrier, count = mesh_barrier(col, cols, row, rows)
-    cost[...] = volume_ref[...].astype(jnp.float32)
-    acc[...] = jnp.zeros_like(acc)
+    span = NDISP // tile_rows
+    groups = tile_cols // span
+    vreg = (SUBS, NDISP)
+    sub = lax.broadcasted_iota(jnp.int32, vreg, 0)
+    lane = lax.broadcasted_iota(jnp.int32, vreg, 1)
+    first_edge = jnp.where(sub == 0, BIG_VALUE, 0.0)
+    last_edge = jnp.where(sub == SUBS - 1, BIG_VALUE, 0.0)
+    near_row = lax.broadcasted_iota(jnp.int32, (NDISP, NDISP), 0)
+    near_col = lax.broadcasted_iota(jnp.int32, (NDISP, NDISP), 1)
+    order = ((near_row % SUBS) * LEADS + near_row // SUBS == near_col).astype(jnp.float32)
+    order = order.astype(jnp.bfloat16)
+
+    def ordered(block):
+        return lax.dot_general(
+            order, block, (((1,), (1,)), ((), ())), preferred_element_type=jnp.float32
+        )
+
+    def restored(block):
+        turned = block.T
+        high = turned.astype(jnp.bfloat16)
+        low = (turned - high.astype(jnp.float32)).astype(jnp.bfloat16)
+        return jnp.dot(high, order, preferred_element_type=jnp.float32) + jnp.dot(
+            low, order, preferred_element_type=jnp.float32
+        )
+
+    def spread(group, carried):
+        start = pl.multiple_of(group * span, span)
+        block = jnp.concatenate(
+            [volume_ref[y, pl.ds(start, span), :] for y in range(tile_rows)], axis=0
+        )
+        block = ordered(block)
+        for lead in range(LEADS):
+            piece = block[lead * SUBS : lead * SUBS + SUBS]
+            for x in range(span):
+                h_cost[start + x, lead] = pltpu.roll(piece, (NDISP - x) % NDISP, 1)
+        return carried
+
+    lax.fori_loop(0, groups, spread, 0)
     pl.semaphore_wait(barrier, count)
 
-    def edges(shape):
-        lane = lax.broadcasted_iota(jnp.int32, shape, 1)
-        low_edge = jnp.where(lane == 0, BIG_VALUE, PENALTY_SMALL)
-        high_edge = jnp.where(lane == NDISP - 1, BIG_VALUE, PENALTY_SMALL)
-        return low_edge, high_edge
-
-    def near(state, low_edge, high_edge):
-        return jnp.minimum(
-            state,
-            jnp.minimum(
-                pltpu.roll(state, 1, 1) + low_edge, pltpu.roll(state, NDISP - 1, 1) + high_edge
-            ),
-        )
+    def advance(state, here):
+        lowest = list(state)
+        while len(lowest) > 1:
+            lowest = [jnp.minimum(lowest[i], lowest[i + 1]) for i in range(0, len(lowest), 2)]
+        lowest = lowest[0]
+        for shift in (4, 2, 1):
+            lowest = jnp.minimum(lowest, pltpu.roll(lowest, shift, 0))
+        below = jnp.maximum(pltpu.roll(state[LEADS - 1], 1, 0), first_edge)
+        above = jnp.maximum(pltpu.roll(state[0], SUBS - 1, 0), last_edge)
+        ext = [below, *state, above]
+        new = []
+        for lead in range(LEADS):
+            near = jnp.minimum(
+                state[lead], jnp.minimum(ext[lead], ext[lead + 2]) + PENALTY_SMALL
+            )
+            new.append(
+                jnp.minimum(near + here[lead], lowest + (here[lead] + PENALTY_LARGE))
+            )
+        return tuple(new), lowest
 
     def run(axis, place, size, backward, send, recv, send_sem, recv_sem, sweep):
         way = backward.astype(jnp.int32)
@@ -161,7 +210,7 @@
         def _():
             recv[way] = jnp.zeros(recv.shape[1:], jnp.float32)
 
-        send[way] = sweep(recv[way], backward)
+        sweep(way, backward)
 
         @pl.when(has_target)
         def _():
@@ -169,43 +218,41 @@
 
         return copy, has_target
 
-    def row_sweep(state, backward):
-        low_edge, high_edge = edges(state.shape)
+    def row_sweep(way, backward):
+        packed = h_recv[way]
+        state = tuple(pltpu.roll(packed, (NDISP - i) % NDISP, 1) for i in range(LEADS))
+
+        def body(index, carried):
+            place = jnp.where(backward, tile_cols - 1 - index, index)
+            here = [h_cost[place, lead] for lead in range(LEADS)]
+            state, lowest = advance(carried[0], here)
+            for lead in range(LEADS):
+                h_path[way, place, lead] = state[lead] - lowest
+            return state, lowest
+
+        state, lowest = lax.fori_loop(
+            0, tile_cols, body, (state, jnp.zeros(vreg, jnp.float32)), unroll=2
+        )
+        packed = state[0] - lowest
+        for lead in range(1, LEADS):
+            moved = pltpu.roll(state[lead] - lowest, lead, 1)
+            packed = jnp.where(lane % span == lead, moved, packed)
+        h_send[way] = packed
+
+    def column_sweep(way, backward):
+        state = tuple(v_recv[way, lead] for lead in range(LEADS))
 
         def body(index, state):
-            place = jnp.where(backward, tile_cols - 1 - index, index)
-            where = pl.ds(place, tile_rows, stride=tile_cols)
-            here = cost[where, :]
-            lowest = jnp.min(state, axis=1, keepdims=True)
-            updated = jnp.minimum(
-                near(state, low_edge, high_edge) + here, lowest + (here + PENALTY_LARGE)
-            )
-            acc[where, :] = acc[where, :] + (updated - lowest)
-            return updated
-
-        state = lax.fori_loop(0, tile_cols, body, state, unroll=4)
-        return state - jnp.min(state, axis=1, keepdims=True)
-
-    def column_sweep(state, backward):
-        low_edge, high_edge = edges((8, NDISP))
-
-        def body(index, carried):
             place = jnp.where(backward, tile_rows - 1 - index, index)
-            new = []
-            for piece, state in enumerate(carried):
-                where = pl.ds(pl.multiple_of(place * tile_cols + piece * 8, 8), 8)
-                lowest = jnp.min(state, axis=1, keepdims=True)
-                updated = (
-                    jnp.minimum(near(state, low_edge, high_edge), lowest + PENALTY_LARGE)
-                    - lowest
-                    + cost[where, :]
-                )
-                acc[where, :] = acc[where, :] + updated
-                new.append(updated)
-            return tuple(new)
-
-        pieces = tuple(state[i * 8 : i * 8 + 8] for i in range(tile_cols // 8))
-        return jnp.concatenate(lax.fori_loop(0, tile_rows, body, pieces), axis=0)
+            here = [v_cost[place, lead] for lead in range(LEADS)]
+            state, lowest = advance(state, here)
+            for lead in range(LEADS):
+                v_path[way, place, lead] = state[lead] - lowest
+            return tuple(value - lowest for value in state)
+
+        state = lax.fori_loop(0, tile_rows, body, state)
+        for lead in range(LEADS):
+            v_send[way, lead] = state[lead]
 
     def horizontal(turn):
         right_half = col > cols - 1 - col
@@ -215,6 +262,14 @@
         )
 
     def vertical():
+        def place_row(y, carried):
+            block = ordered(volume_ref[y])
+            for lead in range(LEADS):
+                v_cost[y, lead] = block[lead * SUBS : lead * SUBS + SUBS]
+            return carried
+
+        lax.fori_loop(0, tile_rows, place_row, 0)
+
         def one(turn, carried):
             lower_half = row > rows - 1 - row
             backward = lower_half != (turn == 1)
@@ -230,6 +285,15 @@
 
         lax.fori_loop(0, 2, one, 0)
 
+        def gather_row(y, carried):
+            block = jnp.concatenate(
+                [v_path[0, y, lead] + v_path[1, y, lead] for lead in range(LEADS)], axis=0
+            )
+            total[y] = restored(block)
+            return carried
+
+        lax.fori_loop(0, tile_rows, gather_row, 0)
+
     late = 2 * jnp.minimum(col, cols - 1 - col) >= cols // 2
 
     @pl.when(late)
@@ -243,7 +307,25 @@
         vertical()
 
     second, second_sent = horizontal(1)
-    out_ref[...] = (acc[...] * 0.25).astype(jnp.bfloat16)
+
+    def gather(group, carried):
+        start = pl.multiple_of(group * span, span)
+        pieces = []
+        for lead in range(LEADS):
+            merged = h_path[0, start, lead] + h_path[1, start, lead]
+            for x in range(1, span):
+                moved = pltpu.roll(h_path[0, start + x, lead] + h_path[1, start + x, lead], x, 1)
+                merged = jnp.where(lane % span == x, moved, merged)
+            pieces.append(merged)
+        block = restored(jnp.concatenate(pieces, axis=0))
+        for y in range(tile_rows):
+            where = pl.ds(start, span)
+            out_ref[y, where, :] = (
+                (total[y, where, :] + block[y * span : y * span + span]) * 0.25
+            ).astype(jnp.bfloat16)
+        return carried
+
+    lax.fori_loop(0, groups, gather, 0)
 
     @pl.when(first_sent)
     def _():
@@ -256,28 +338,32 @@
 
 def aggregate(volume):
     tile_rows, tile_cols, disps = volume.shape
-    count = tile_rows * tile_cols
-    out = pl.pallas_call(
+    vregs = (LEADS, SUBS, NDISP)
+    return pl.pallas_call(
         partial(path_kernel, tile_rows, tile_cols),
-        out_shape=jax.ShapeDtypeStruct((count, disps), jnp.bfloat16),
+        out_shape=jax.ShapeDtypeStruct(volume.shape, jnp.bfloat16),
         in_specs=[pl.BlockSpec(memory_space=pltpu.VMEM)],
         out_specs=pl.BlockSpec(memory_space=pltpu.VMEM),
         scratch_shapes=[
-            pltpu.VMEM((count, disps), jnp.float32),
-            pltpu.VMEM((count, disps), jnp.float32),
-            pltpu.VMEM((2, tile_rows, disps), jnp.float32),
-            pltpu.VMEM((2, tile_rows, disps), jnp.float32),
-            pltpu.VMEM((2, tile_cols, disps), jnp.float32),
-            pltpu.VMEM((2, tile_cols, disps), jnp.float32),
+            pltpu.VMEM((tile_rows, *vregs), jnp.float32),
+            pltpu.VMEM((tile_cols, *vregs), jnp.float32),
+            pltpu.VMEM((2, tile_cols, *vregs), jnp.float32),
+            pltpu.VMEM((2, tile_rows, *vregs), jnp.float32),
+            pltpu.VMEM(volume.shape, jnp.float32),
+            pltpu.VMEM((2, SUBS, NDISP), jnp.float32),
+            pltpu.VMEM((2, SUBS, NDISP), jnp.float32),
+            pltpu.VMEM((2, *vregs), jnp.float32),
+            pltpu.VMEM((2, *vregs), jnp.float32),
             pltpu.SemaphoreType.DMA((2,)),
             pltpu.SemaphoreType.DMA((2,)),
             pltpu.SemaphoreType.DMA((2,)),
             pltpu.SemaphoreType.DMA((2,)),
         ],
-        compiler_params=pltpu.CompilerParams(collective_id=0, has_side_effects=True),
+        compiler_params=pltpu.CompilerParams(
+            collective_id=0, has_side_effects=True, vmem_limit_bytes=48 << 20
+        ),
         name="paths",
-    )(volume.reshape(count, disps))
-    return out.reshape(tile_rows, tile_cols, disps)
+    )(volume)
 
 
 def on_device(

time: 160 us -> 104 us (0.65)
  Pallas kernels: 106 us -> 51.8 us
    pallas_call x1, Pallas kernels: 106 us -> 51.8 us  [aggregate(): pl.pallas_call(partial(path_kernel, tile_rows, tile_cols), out_shape=jax....]
  transfers between devices with their start and end apart: 5 -> 5, of which waited for: 1 -> 1; matrix products, arithmetic and copies ran while one was open for 5% -> 8% of each run, Pallas kernels for 0% -> 0%
where the time goes in v2:
time: 104 us
  Pallas kernels  51.8 us (50%)
  local copies, waits for them, and re-layouts  26.7 us (26%)
  starting transfers between devices  15.9 us (15%)
  other arithmetic  3.22 us (3%)
  matrix products  2.79 us (3%)
  between operations  1.96 us (2%)
  waiting for transfers between devices  1.31 us (1%)
    pallas_call x1, Pallas kernels, aggregate(): pl.pallas_call(partial(path_kernel, tile_rows, tile_cols), out_shape=jax....  51.8 us
    unnamed x41, local copies, waits for them, and re-layouts  11.6 us
    ppermute x2, starting transfers between devices, padded(): before = lax.ppermute(last, axis, up)  8.53 us
    reshape x2, local copies, waits for them, and re-layouts, conv_valid(): patches = jnp.stack(pieces, 0).reshape(9 * in_chan, out_rows * out_cols)  6.98 us
    ppermute x1, starting transfers between devices, passed_along(): lax.ppermute(value, axis, [(source, source + steps) for source in range(i...  4.82 us
    another operation x24, local copies, waits for them, and re-layouts, conv_valid(): patches = jnp.stack(pieces, 0).reshape(9 * in_chan, out_rows * out_cols)  3.71 us
    ppermute x2, starting transfers between devices, padded(): after = lax.ppermute(initial, axis, down)  2.57 us
    dot_general x6, matrix products, conv_valid(): result = jnp.dot(weight, patches, preferred_element_type=jnp.float32)  2.42 us
  transfers between devices with their start and end apart: 5, of which 1 were waited for; matrix products, arithmetic and copies ran while one was open for 8% of the time, Pallas kernels for 0%

profile of v2, /device:TPU:0, one launch (start us, length us, event | category | flops | bytes accessed | tf_op | source)
XLA Modules:
  0.0 103.7 jit_solution(2205553199951012621)
XLA Ops:
  0.0 0.8 fusion.45
  0.8 1.3 %collective-permute-start.1 = (bf16[2,3,128]{2,1,0:T(4,128)(2,1)S(1)}, bf16[2,3,128]{2,1,0:T(4,128)(2,1)S(1)}, u32[]{:S(2)}, u32[]{:S(2)}) collective-permute-start(bf16[2,3,128]{2,1,0:T(4,128)(2,1)S(1)} %get-tuple-element.26), channel_id=1, source_target_pairs={{8,0},{16,8},{24,16},{9,1},{17,9},{25,17},{10,2},{18,10},{26,18},{... | collective-permute-start | bytes 4616 | tf_op jit(solution)/shard_map/ppermute | solution.py:28
  2.1 3.0 %collective-permute-start = (bf16[2,3,128]{2,1,0:T(4,128)(2,1)S(1)}, bf16[2,3,128]{2,1,0:T(4,128)(2,1)S(1)}, u32[]{:S(2)}, u32[]{:S(2)}) collective-permute-start(bf16[2,3,128]{2,1,0:T(4,128)(2,1)S(1)} %get-tuple-element.25), channel_id=1, source_target_pairs={{0,8},{8,16},{16,24},{1,9},{9,17},{17,25},{2,10},{10,18},{18,26},{... | collective-permute-start | bytes 4616 | tf_op jit(solution)/shard_map/ppermute | solution.py:27
  7.2 0.7 pad_maximum_fusion.1
  8.0 1.3 %collective-permute-start.3 = (bf16[2,14,3]{2,1,0:T(8,128)(2,1)S(1)}, bf16[2,14,3]{2,1,0:T(8,128)(2,1)S(1)}, u32[]{:S(2)}, u32[]{:S(2)}) collective-permute-start(bf16[2,14,3]{2,1,0:T(8,128)(2,1)S(1)} %get-tuple-element.24), channel_id=1, source_target_pairs={{1,0},{2,1},{3,2},{4,3},{5,4},{6,5},{7,6},{9,8},{10,9},{11,10},{12... | collective-permute-start | bytes 512 | tf_op jit(solution)/shard_map/ppermute | solution.py:28
  9.3 5.5 %collective-permute-start.2 = (bf16[2,14,3]{2,1,0:T(8,128)(2,1)S(1)}, bf16[2,14,3]{2,1,0:T(8,128)(2,1)S(1)}, u32[]{:S(2)}, u32[]{:S(2)}) collective-permute-start(bf16[2,14,3]{2,1,0:T(8,128)(2,1)S(1)} %get-tuple-element.23), channel_id=1, source_target_pairs={{0,1},{1,2},{2,3},{3,4},{4,5},{5,6},{6,7},{8,9},{9,10},{10,11},{11... | collective-permute-start | bytes 512 | tf_op jit(solution)/shard_map/ppermute | solution.py:27
  14.8 1.3 %collective-permute-done.2 = bf16[2,14,3]{2,1,0:T(8,128)(2,1)S(1)} collective-permute-done((bf16[2,14,3]{2,1,0:T(8,128)(2,1)S(1)}, bf16[2,14,3]{2,1,0:T(8,128)(2,1)S(1)}, u32[]{:S(2)}, u32[]{:S(2)}) %collective-permute-start.2) | collective-permute-done | bytes 200 | tf_op jit(solution)/shard_map/ppermute | solution.py:27
  16.1 0.8 pad_maximum_fusion
  17.0 4.8 %collective-permute-start.4 = (bf16[14,134]{1,0:T(8,128)(2,1)S(1)}, bf16[14,134]{1,0:T(8,128)(2,1)S(1)}, u32[]{:S(2)}, u32[]{:S(2)}) collective-permute-start(bf16[14,134]{1,0:T(8,128)(2,1)S(1)} %slice_bitcast_fusion.36), channel_id=1, source_target_pairs={{0,1},{1,2},{2,3},{3,4},{4,5},{5,6},{6,7},{8,9},{9,10},{10,11},{11... | collective-permute-start | bytes 11264 | tf_op jit(solution)/shard_map/ppermute | solution.py:36
  21.9 0.1 stack.193
  22.8 0.1 stack.201
  22.9 0.9 fusion.2
  23.8 0.5 max.85
  24.5 0.1 fusion.25
  24.6 0.1 fusion.24
  24.9 0.2 fusion.22
  25.1 0.2 fusion.21
  25.3 0.2 fusion.19
  25.5 0.2 fusion.18
  25.8 2.4 %reshape.331 = bf16[288,1300]{1,0:T(8,128)(2,1)S(1)} reshape(bf16[9,32,10,130]{3,2,1,0:T(8,128)(2,1)S(1)} %fusion.18) | data formatting | bytes 1497600 | tf_op jit(solution)/shard_map/reshape | solution.py:48
  28.2 0.3 fusion.3
  28.4 0.5 max.90
  29.2 0.1 constant_dynamic-update-slice_fusion.4
  29.4 0.1 constant_dynamic-update-slice_fusion.3
  29.5 0.1 constant_dynamic-update-slice_fusion.1
  29.7 0.1 constant_dynamic-update-slice_fusion
  29.8 0.2 multiply_reduce_fusion.1
  30.2 0.1 stack.222
  30.3 0.1 stack.223
  30.4 0.1 stack.224
  30.6 0.1 stack.225
  30.7 0.1 stack.226
  30.8 0.1 stack.227
  30.9 0.1 stack.228
  31.0 0.1 stack.229
  31.1 0.1 stack.230
  31.3 0.2 stack.231
  31.5 0.3 fusion
  31.7 0.4 max.95
  32.2 0.8 fusion.16
  33.0 1.0 fusion.15
  34.0 1.0 fusion.14
  34.9 0.9 fusion.13
  35.8 1.0 fusion.12
  36.8 1.0 fusion.11
  37.8 0.9 fusion.10
  38.7 1.0 fusion.9
  39.7 1.0 fusion.8
  40.7 4.6 %reshape.334 = bf16[288,2580]{1,0:T(8,128)(2,1)S(1)} reshape(bf16[9,32,10,258]{3,2,1,0:T(8,128)(2,1)} %fusion.8) | data formatting | bytes 2972160 | tf_op jit(solution)/shard_map/reshape | solution.py:48
  45.3 0.4 fusion.1
  45.7 0.3 max.100
  46.4 0.1 fusion.34
  46.6 0.1 fusion.33
  46.8 0.1 fusion.31
  46.9 0.1 fusion.30
  47.1 0.3 copy.15
  47.4 0.4 multiply_reduce_fusion
  47.8 0.4 fusion.4
  48.2 0.6 copy.16
  48.9 1.3 %reshape.338 = f32[8,128,257]{2,1,0:T(8,128)S(1)} reshape(f32[8,32896]{1,0:T(8,128)S(1)} %pad.4) | data formatting | bytes 2105344 | tf_op jit(solution)/shard_map/reshape | solution.py:81
  50.2 0.2 slice.315
  50.4 0.7 rev.3
  51.2 51.8 %paths.1 = bf16[8,128,128]{2,1,0:T(8,128)(2,1)S(1)} custom-call(bf16[8,128,128]{2,1,0:T(8,128)(2,1)S(1)} %select_convert_fusion.2.volume_ref), custom_call_target="tpu_custom_call" | custom-call | tf_op jit(solution)/shard_map/paths/pallas_call | solution.py:342
  103.0 0.7 copy.62
  (68 shorter events, 3.1 us)
Async XLA Ops:
  0.0 28.2 %copy-start = (bf16[32,288]{1,0:T(8,128)(2,1)S(1)}, bf16[32,288]{1,0:T(8,128)(2,1)}, u32[]{:S(2)}) copy-start(bf16[32,288]{1,0:T(8,128)(2,1)} %param.10) | copy-start | bytes 55300
  0.8 6.4 %collective-permute-start.1 = (bf16[2,3,128]{2,1,0:T(4,128)(2,1)S(1)}, bf16[2,3,128]{2,1,0:T(4,128)(2,1)S(1)}, u32[]{:S(2)}, u32[]{:S(2)}) collective-permute-start(bf16[2,3,128]{2,1,0:T(4,128)(2,1)S(1)} %get-tuple-element.26), channel_id=1, source_target_pairs={{8,0},{16,8},{24,16},{9,1},{17,9},{25,17},{10,2},{18,10},{26,18},{... | collective-permute-start | bytes 4616 | tf_op jit(solution)/shard_map/ppermute | solution.py:28
  2.1 5.1 %collective-permute-start = (bf16[2,3,128]{2,1,0:T(4,128)(2,1)S(1)}, bf16[2,3,128]{2,1,0:T(4,128)(2,1)S(1)}, u32[]{:S(2)}, u32[]{:S(2)}) collective-permute-start(bf16[2,3,128]{2,1,0:T(4,128)(2,1)S(1)} %get-tuple-element.25), channel_id=1, source_target_pairs={{0,8},{8,16},{16,24},{1,9},{9,17},{17,25},{2,10},{10,18},{18,26},{... | collective-permute-start | bytes 4616 | tf_op jit(solution)/shard_map/ppermute | solution.py:27
  8.0 6.8 %collective-permute-start.3 = (bf16[2,14,3]{2,1,0:T(8,128)(2,1)S(1)}, bf16[2,14,3]{2,1,0:T(8,128)(2,1)S(1)}, u32[]{:S(2)}, u32[]{:S(2)}) collective-permute-start(bf16[2,14,3]{2,1,0:T(8,128)(2,1)S(1)} %get-tuple-element.24), channel_id=1, source_target_pairs={{1,0},{2,1},{3,2},{4,3},{5,4},{6,5},{7,6},{9,8},{10,9},{11,10},{12... | collective-permute-start | bytes 512 | tf_op jit(solution)/shard_map/ppermute | solution.py:28
  9.3 6.9 %collective-permute-start.2 = (bf16[2,14,3]{2,1,0:T(8,128)(2,1)S(1)}, bf16[2,14,3]{2,1,0:T(8,128)(2,1)S(1)}, u32[]{:S(2)}, u32[]{:S(2)}) collective-permute-start(bf16[2,14,3]{2,1,0:T(8,128)(2,1)S(1)} %get-tuple-element.23), channel_id=1, source_target_pairs={{0,1},{1,2},{2,3},{3,4},{4,5},{5,6},{6,7},{8,9},{9,10},{10,11},{11... | collective-permute-start | bytes 512 | tf_op jit(solution)/shard_map/ppermute | solution.py:27
  17.0 13.1 %collective-permute-start.4 = (bf16[14,134]{1,0:T(8,128)(2,1)S(1)}, bf16[14,134]{1,0:T(8,128)(2,1)S(1)}, u32[]{:S(2)}, u32[]{:S(2)}) collective-permute-start(bf16[14,134]{1,0:T(8,128)(2,1)S(1)} %slice_bitcast_fusion.36), channel_id=1, source_target_pairs={{0,1},{1,2},{2,3},{3,4},{4,5},{5,6},{6,7},{8,9},{9,10},{10,11},{11... | collective-permute-start | bytes 11264 | tf_op jit(solution)/shard_map/ppermute | solution.py:36
  25.7 4.1 %copy-start.1 = (bf16[32,288]{1,0:T(8,128)(2,1)S(1)}, bf16[32,288]{1,0:T(8,128)(2,1)}, u32[]{:S(2)}) copy-start(bf16[32,288]{1,0:T(8,128)(2,1)} %param.11) | copy-start | bytes 55300
  28.2 3.3 %copy-start.2 = (bf16[32,9]{0,1:T(8,128)(2,1)S(1)}, bf16[32,9]{0,1:T(8,128)(2,1)}, u32[]{:S(2)}) copy-start(bf16[32,9]{0,1:T(8,128)(2,1)} %param.9) | copy-start | bytes 1732

commit v3 on v2

--- a/solution.py
+++ b/solution.py
@@ -17,72 +17,178 @@
 BIG_VALUE = 1e30
 
 
-def padded(x, sides, width):
-    for axis, dim in sides:
-        size, length = (lax.axis_size(axis), x.shape[dim])
-        up = [(i, (i + 1) % size) for i in range(size - 1)]
-        down = [(j, i) for i, j in up]
-        last = lax.slice_in_dim(x, length - width, length, axis=dim)
-        initial = lax.slice_in_dim(x, 0, width, axis=dim)
-        before = lax.ppermute(last, axis, up)
-        after = lax.ppermute(initial, axis, down)
-        x = jnp.concatenate([before, x, after], axis=dim)
-    return x
-
-
-def passed_along(value, axis, steps):
-    count = lax.axis_size(axis)
-    initial, last = (max(0, -steps), min(count, count - steps))
-    return lax.ppermute(value, axis, [(source, source + steps) for source in range(initial, last)])
-
-
-def conv_valid(source, weight):
-    in_chan, ext_rows, ext_cols = source.shape
-    out_rows = ext_rows - 2
-    out_cols = ext_cols - 2
-    pieces = [
-        source[:, row_off : row_off + out_rows, col_off : col_off + out_cols]
-        for row_off in range(3)
-        for col_off in range(3)
+ROW_BLOCKS = 3
+COL_BLOCKS = 4
+
+
+def exchange_kernel(own_ref, out_ref, send_sem, recv_sem):
+    cols, rows = lax.axis_size("col"), lax.axis_size("row")
+    col, row = lax.axis_index("col"), lax.axis_index("row")
+    barrier = pltpu.get_barrier_semaphore()
+    moves = [
+        (down, right)
+        for down in (-1, 0, 1)
+        for right in (-1, 0, 1, 2)
+        if (down, right) != (0, 0)
     ]
-    patches = jnp.stack(pieces, 0).reshape(9 * in_chan, out_rows * out_cols)
-    result = jnp.dot(weight, patches, preferred_element_type=jnp.float32)
-    return result.reshape(weight.shape[0], out_rows, out_cols)
-
-
-def tower_valid(source, weights, first_row, first_col, total_rows, total_cols):
-    current = source[None]
-    for layer_num in range(3):
-        result = conv_valid(current, weights[layer_num])
-        if layer_num < 2:
-            result = jnp.maximum(result, 0.0)
-        row_place = first_row + layer_num + 1 + jnp.arange(result.shape[1])
-        col_place = first_col + layer_num + 1 + jnp.arange(result.shape[2])
-        inside = ((row_place >= 0) & (row_place < total_rows))[:, None] & (
-            (col_place >= 0) & (col_place < total_cols)
-        )[None, :]
-        current = jnp.where(inside[None], result, 0.0).astype(jnp.bfloat16)
-    return current
-
-
-def feature_norm(features):
-    return jnp.maximum(jnp.sqrt(jnp.sum(jnp.square(features.astype(jnp.float32)), axis=0)), 1.0)
-
-
-def correlate(left_feat, right_ext, base_disp, range_width):
-    chans, tile_rows, tile_cols = left_feat.shape
-    left_norm = feature_norm(left_feat)
-    right_norm = feature_norm(right_ext)
-    products = jnp.einsum("cyx,cyz->yxz", left_feat, right_ext, preferred_element_type=jnp.float32)
-    cosine = products / (left_norm[:, :, None] * right_norm[:, None, :])
-    ext_span = 2 * tile_cols
-    flattened = cosine.reshape(tile_rows, tile_cols * ext_span)
-    flattened = jnp.pad(flattened, ((0, 0), (0, tile_cols)))
-    skewed = flattened.reshape(tile_rows, tile_cols, ext_span + 1)
-    diagonal_band = skewed[:, :, tile_cols - NDISP + 1 : tile_cols + 1][:, :, ::-1]
-    shifts = jnp.arange(NDISP)
-    in_range = (shifts >= base_disp) & (shifts < base_disp + range_width)
-    return jnp.where(in_range, 1.0 - diagonal_band, INVALID_COST).astype(jnp.bfloat16)
+
+    def exists(down, right):
+        return (
+            (row + down >= 0) & (row + down < rows) & (col + right >= 0) & (col + right < cols)
+        )
+
+    count = jnp.int32(0)
+    for down, right in moves:
+
+        @pl.when(exists(-down, -right))
+        def _():
+            pl.semaphore_signal(
+                barrier,
+                inc=1,
+                device_id={"row": row - down, "col": col - right},
+                device_id_type=MESH,
+            )
+
+        count = count + exists(down, right).astype(jnp.int32)
+    out_ref[1, 2] = own_ref[...]
+    pl.semaphore_wait(barrier, count)
+
+    def copy_of(down, right):
+        return pltpu.make_async_remote_copy(
+            src_ref=own_ref,
+            dst_ref=out_ref.at[1 - down, 2 - right],
+            send_sem=send_sem.at[1 - down, 2 - right],
+            recv_sem=recv_sem.at[1 - down, 2 - right],
+            device_id={"row": row + down, "col": col + right},
+            device_id_type=MESH,
+        )
+
+    for down, right in moves:
+
+        @pl.when(exists(down, right))
+        def _():
+            copy_of(down, right).start()
+
+        @pl.when(jnp.logical_not(exists(-down, -right)))
+        def _():
+            out_ref[1 - down, 2 - right] = jnp.zeros(own_ref.shape, jnp.float32)
+
+    for down, right in moves:
+
+        @pl.when(exists(-down, -right))
+        def _():
+            copy_of(down, right).wait_recv()
+
+        @pl.when(exists(down, right))
+        def _():
+            copy_of(down, right).wait_send()
+
+
+def exchange(images):
+    shape = (ROW_BLOCKS, COL_BLOCKS, *images.shape)
+    return pl.pallas_call(
+        exchange_kernel,
+        out_shape=jax.ShapeDtypeStruct(shape, jnp.float32),
+        in_specs=[pl.BlockSpec(memory_space=pltpu.VMEM)],
+        out_specs=pl.BlockSpec(memory_space=pltpu.VMEM),
+        scratch_shapes=[
+            pltpu.SemaphoreType.DMA((ROW_BLOCKS, COL_BLOCKS)),
+            pltpu.SemaphoreType.DMA((ROW_BLOCKS, COL_BLOCKS)),
+        ],
+        compiler_params=pltpu.CompilerParams(collective_id=1, has_side_effects=True),
+        name="exchange",
+    )(images)
+
+
+def layer(source, weight, span, out_rows, rectify, inside):
+    chans, length = source.shape
+    stacked = jnp.concatenate(
+        [pltpu.roll(source, 1, 1), source, pltpu.roll(source, length - 1, 1)], axis=0
+    ).astype(jnp.bfloat16)
+    result = jnp.zeros((weight.shape[0], out_rows * span), jnp.float32)
+    for row_off in range(3):
+        result = result + jnp.dot(
+            weight[:, row_off * 3 * chans : (row_off + 1) * 3 * chans],
+            stacked[:, row_off * span : (row_off + out_rows) * span],
+            preferred_element_type=jnp.float32,
+        )
+    if rectify:
+        result = jnp.maximum(result, 0.0)
+    return jnp.where(inside, result, 0.0).astype(jnp.bfloat16).astype(jnp.float32)
+
+
+def cost_kernel(
+    tile_rows, tile_cols, place_ref, blocks_ref, first_ref, second_ref, third_ref, out_ref
+):
+    base, width = place_ref[0], place_ref[1]
+    first_row, first_col = place_ref[2], place_ref[3]
+    total_rows, total_cols = place_ref[4], place_ref[5]
+    weights = (first_ref[...], second_ref[...], third_ref[...])
+
+    def tower(image, blocks):
+        span = len(blocks) * tile_cols
+        lines = [
+            jnp.concatenate([blocks_ref[0, j, image] for j in blocks], axis=1)[
+                tile_rows - 3 : tile_rows
+            ],
+            jnp.concatenate([blocks_ref[1, j, image] for j in blocks], axis=1),
+            jnp.concatenate([blocks_ref[2, j, image] for j in blocks], axis=1)[0:3],
+        ]
+        current = jnp.concatenate(
+            [line[i : i + 1] for line in lines for i in range(line.shape[0])], axis=1
+        )
+        for num in range(3):
+            out_rows = tile_rows + 4 - 2 * num
+            index = lax.broadcasted_iota(jnp.int32, (1, out_rows * span), 1)
+            row_place = first_row - 2 + num + index // span
+            col_place = first_col + (blocks[0] - 2) * tile_cols + index % span
+            inside = (
+                (row_place >= 0)
+                & (row_place < total_rows)
+                & (col_place >= 0)
+                & (col_place < total_cols)
+            )
+            current = layer(current, weights[num], span, out_rows, num < 2, inside)
+        return current, span
+
+    left, left_span = tower(0, (1, 2, 3))
+    right, right_span = tower(1, (0, 1, 2, 3))
+    ext = 2 * tile_cols
+    flip = lax.broadcasted_iota(jnp.int32, (ext, ext), 0) + lax.broadcasted_iota(
+        jnp.int32, (ext, ext), 1
+    )
+    flip = (flip == ext - 1).astype(jnp.float32).astype(jnp.bfloat16)
+    shifts = lax.broadcasted_iota(jnp.int32, (tile_cols, NDISP), 1)
+    in_range = (shifts >= base) & (shifts < base + width)
+    for y in range(tile_rows):
+        own = left[:, y * left_span + tile_cols : y * left_span + 2 * tile_cols].T
+        other = right[:, y * right_span + tile_cols : y * right_span + 3 * tile_cols]
+        other = jnp.dot(other.astype(jnp.bfloat16), flip, preferred_element_type=jnp.float32)
+        own_norm = jnp.maximum(jnp.sqrt(jnp.sum(own * own, axis=1, keepdims=True)), 1.0)
+        other_norm = jnp.maximum(jnp.sqrt(jnp.sum(other * other, axis=0, keepdims=True)), 1.0)
+        products = jnp.dot(
+            own.astype(jnp.bfloat16),
+            other.astype(jnp.bfloat16),
+            preferred_element_type=jnp.float32,
+        )
+        cosine = products / (own_norm * other_norm)
+        cosine = pltpu.roll(cosine, ext - tile_cols + 1, 1, stride=1, stride_axis=0)
+        out_ref[y] = jnp.where(in_range, 1.0 - cosine[:, :NDISP], INVALID_COST).astype(
+            jnp.bfloat16
+        )
+
+
+def cost_volume(place, blocks, weights):
+    tile_rows, tile_cols = blocks.shape[3:]
+    return pl.pallas_call(
+        partial(cost_kernel, tile_rows, tile_cols),
+        out_shape=jax.ShapeDtypeStruct((tile_rows, tile_cols, NDISP), jnp.bfloat16),
+        in_specs=[pl.BlockSpec(memory_space=pltpu.SMEM)]
+        + [pl.BlockSpec(memory_space=pltpu.VMEM)] * 4,
+        out_specs=pl.BlockSpec(memory_space=pltpu.VMEM),
+        compiler_params=pltpu.CompilerParams(vmem_limit_bytes=32 << 20),
+        name="costs",
+    )(place, blocks, *weights)
 
 
 def mesh_barrier(col, cols, row, rows):
@@ -371,19 +477,19 @@
 ):
     weights = (first_weight, second_weight, third_weight)
     tile_rows, tile_cols = left_image.shape
-    margins = padded(jnp.stack([left_image, right_image]), (("row", 1), ("col", 2)), 3)
-    total_rows = tile_rows * lax.axis_size("row")
-    total_cols = tile_cols * lax.axis_size("col")
-    first_row = lax.axis_index("row") * tile_rows - 3
-    first_col = lax.axis_index("col") * tile_cols - 3
-    left_feat = tower_valid(margins[0], weights, first_row, first_col, total_rows, total_cols)
-    neighbour = passed_along(margins[1], "col", 1)
-    joined = jnp.concatenate([neighbour[:, :tile_cols], margins[1]], axis=1)
-    right_ext = tower_valid(
-        joined, weights, first_row, first_col - tile_cols, total_rows, total_cols
+    rows, cols = lax.axis_size("row"), lax.axis_size("col")
+    blocks = exchange(jnp.stack([left_image, right_image]).astype(jnp.float32))
+    place = jnp.stack(
+        [
+            tile_base[0, 0],
+            tile_width[0, 0],
+            lax.axis_index("row") * tile_rows,
+            lax.axis_index("col") * tile_cols,
+            jnp.int32(rows * tile_rows),
+            jnp.int32(cols * tile_cols),
+        ]
     )
-    volume = correlate(left_feat, right_ext, tile_base[0, 0], tile_width[0, 0])
-    return aggregate(volume)
+    return aggregate(cost_volume(place, blocks, weights))
 
 
 def solution(mesh):

time: 104 us -> 70.5 us (0.68)
  local copies, waits for them, and re-layouts: 26.7 us -> 2.55 us
  starting transfers between devices: 15.9 us -> 0 us
  Pallas kernels: 51.8 us -> 65.7 us
  matrix products: 2.79 us -> 0 us
  other arithmetic: 3.22 us -> 0.6 us
  waiting for transfers between devices: 1.31 us -> 0 us
    ppermute x5 -> x0, starting transfers between devices: 15.9 us -> none  [the longest x2 8.53 us: padded(): before = lax.ppermute(last, axis, up)]
    pallas_call x0 -> x2, Pallas kernels: none -> 12.8 us  [the longest x1 8.14 us: exchange(): pl.pallas_call(exchange_kernel, out_shape=jax.ShapeDtypeStruct(shape, jnp...]
    unnamed x41 -> x14, local copies, waits for them, and re-layouts: 11.6 us -> 2.47 us
    reshape x3 -> x0, local copies, waits for them, and re-layouts: 8.27 us -> none  [the longest x2 6.98 us: conv_valid(): patches = jnp.stack(pieces, 0).reshape(9 * in_chan, out_rows * out_cols)]
    another operation x24 -> x1, local copies, waits for them, and re-layouts: 3.71 us -> 0.08 us  [on_device(): jnp.stack([tile_base[0, 0], tile_width[0, 0], lax.axis_index('row') * til...]
    dot_general x7 -> x0, matrix products: 2.79 us -> none  [the longest x6 2.42 us: conv_valid(): result = jnp.dot(weight, patches, preferred_element_type=jnp.float32)]
    max x5 -> x0, local copies, waits for them, and re-layouts: 1.77 us -> none  [the longest x4 1.76 us: tower_valid(): result = jnp.maximum(result, 0.0)]
    concatenate x2 -> x0, other arithmetic: 1.49 us -> none  [padded(): x = jnp.concatenate([before, x, after], axis=dim)]
  transfers between devices with their start and end apart: 5 -> 0, of which waited for: 1 -> 0; matrix products, arithmetic and copies ran while one was open for 8% -> 0% of each run, Pallas kernels for 0% -> 0%
where the time goes in v3:
time: 70.5 us; the launch traced here: 70.2 us
  Pallas kernels  65.7 us (93%)
  local copies, waits for them, and re-layouts  2.55 us (4%)
  between operations  1.36 us (2%)
    pallas_call x1, Pallas kernels, aggregate(): pl.pallas_call(partial(path_kernel, tile_rows, tile_cols), out_shape=jax....  52.9 us
    pallas_call x1, Pallas kernels, exchange(): pl.pallas_call(exchange_kernel, out_shape=jax.ShapeDtypeStruct(shape, jnp...  8.14 us
    pallas_call x1, Pallas kernels, cost_volume(): pl.pallas_call(partial(cost_kernel, tile_rows, tile_cols), out_shape=jax....  4.68 us
    unnamed x14, local copies, waits for them, and re-layouts  2.47 us

profile of v3, /device:TPU:0, one launch (start us, length us, event | category | flops | bytes accessed | tf_op | source)
XLA Modules:
  0.0 70.2 jit_solution(6088248675735835219)
XLA Ops:
  1.3 0.0 copy-start.5
  1.3 0.1 stack.20.place_ref
  1.4 0.0 copy-start.4
  1.4 0.6 copy-done.5
  2.0 0.1 copy-done.4
  2.1 0.0 copy-start.3
  2.1 0.6 maximum_convert_fusion.own_ref
  2.7 0.1 copy-done.3
  2.8 0.1 copy.8.first_ref
  2.9 0.0 copy-start.1
  2.9 0.0 copy-start.2
  2.9 8.1 %exchange.1.blocks_ref = f32[3,4,2,8,128]{4,3,2,1,0:T(8,128)} custom-call(f32[2,8,128]{2,1,0:T(8,128)} %maximum_convert_fusion.own_ref), custom_call_target="tpu_custom_call" | custom-call | tf_op jit(solution)/shard_map/exchange/pallas_call | solution.py:89
  11.0 0.0 copy-done.1
  11.0 0.0 copy-done.2
  11.0 0.0 copy-start
  11.0 0.9 %copy-done = f32[3,4,2,8,128]{4,3,2,1,0:T(8,128)S(1)} copy-done((f32[3,4,2,8,128]{4,3,2,1,0:T(8,128)S(1)}, f32[3,4,2,8,128]{4,3,2,1,0:T(8,128)}, u32[]{:S(2)}) %copy-start) | copy-done | bytes 98328
  11.9 4.7 %costs.1.volume_ref = bf16[8,128,128]{2,1,0:T(8,128)(2,1)S(1)} custom-call(s32[6]{0:T(128)S(1)} %stack.20.place_ref, f32[3,4,2,8,128]{4,3,2,1,0:T(8,128)S(1)} %copy-done, bf16[32,9]{1,0:T(8,128)(2,1)S(1)} %copy.8.first_ref, bf16[32,288]{1,0:T(8,128)(2,1)S(1)} %copy-done.1, bf16[32,288]{1,0:T(8,128)(2,1)S(1)} %copy-done.2), custom_call_target="tpu_custom_call" | custom-call | tf_op jit(solution)/shard_map/costs/pallas_call | solution.py:183
  16.6 52.9 %paths.1 = bf16[8,128,128]{2,1,0:T(8,128)(2,1)S(1)} custom-call(bf16[8,128,128]{2,1,0:T(8,128)(2,1)S(1)} %costs.1.volume_ref), custom_call_target="tpu_custom_call" | custom-call | tf_op jit(solution)/shard_map/paths/pallas_call | solution.py:448
  69.5 0.7 %copy.12 = bf16[8,128,128]{2,1,0:T(8,128)(2,1)} copy(bf16[8,128,128]{2,1,0:T(8,128)(2,1)S(1)} %paths.1) | data formatting | bytes 524288
Async XLA Ops:
  1.3 0.7 copy-start.5
  1.4 0.7 copy-start.4
  2.1 0.7 copy-start.3
  2.9 8.1 %copy-start.1 = (bf16[32,288]{1,0:T(8,128)(2,1)S(1)}, bf16[32,288]{1,0:T(8,128)(2,1)}, u32[]{:S(2)}) copy-start(bf16[32,288]{1,0:T(8,128)(2,1)} %second_ref.1) | copy-start | bytes 55300
  2.9 8.2 %copy-start.2 = (bf16[32,288]{1,0:T(8,128)(2,1)S(1)}, bf16[32,288]{1,0:T(8,128)(2,1)}, u32[]{:S(2)}) copy-start(bf16[32,288]{1,0:T(8,128)(2,1)} %third_ref.1) | copy-start | bytes 55300
  11.0 0.9 %copy-start = (f32[3,4,2,8,128]{4,3,2,1,0:T(8,128)S(1)}, f32[3,4,2,8,128]{4,3,2,1,0:T(8,128)}, u32[]{:S(2)}) copy-start(f32[3,4,2,8,128]{4,3,2,1,0:T(8,128)} %exchange.1.blocks_ref) | copy-start | bytes 294916

commit v4 on v3

--- a/solution.py
+++ b/solution.py
@@ -21,7 +21,7 @@
 COL_BLOCKS = 4
 
 
-def exchange_kernel(own_ref, out_ref, send_sem, recv_sem):
+def exchange_kernel(left_ref, right_ref, out_ref, own_ref, send_sem, recv_sem):
     cols, rows = lax.axis_size("col"), lax.axis_size("row")
     col, row = lax.axis_index("col"), lax.axis_index("row")
     barrier = pltpu.get_barrier_semaphore()
@@ -50,7 +50,10 @@
             )
 
         count = count + exists(down, right).astype(jnp.int32)
-    out_ref[1, 2] = own_ref[...]
+    for num, image in enumerate((left_ref, right_ref)):
+        value = image[...].astype(jnp.float32)
+        own_ref[num] = value
+        out_ref[1, 2, num] = value
     pl.semaphore_wait(barrier, count)
 
     def copy_of(down, right):
@@ -84,20 +87,21 @@
             copy_of(down, right).wait_send()
 
 
-def exchange(images):
-    shape = (ROW_BLOCKS, COL_BLOCKS, *images.shape)
+def exchange(left_image, right_image):
+    pair = (2, *left_image.shape)
     return pl.pallas_call(
         exchange_kernel,
-        out_shape=jax.ShapeDtypeStruct(shape, jnp.float32),
-        in_specs=[pl.BlockSpec(memory_space=pltpu.VMEM)],
+        out_shape=jax.ShapeDtypeStruct((ROW_BLOCKS, COL_BLOCKS, *pair), jnp.float32),
+        in_specs=[pl.BlockSpec(memory_space=pltpu.VMEM)] * 2,
         out_specs=pl.BlockSpec(memory_space=pltpu.VMEM),
         scratch_shapes=[
+            pltpu.VMEM(pair, jnp.float32),
             pltpu.SemaphoreType.DMA((ROW_BLOCKS, COL_BLOCKS)),
             pltpu.SemaphoreType.DMA((ROW_BLOCKS, COL_BLOCKS)),
         ],
         compiler_params=pltpu.CompilerParams(collective_id=1, has_side_effects=True),
         name="exchange",
-    )(images)
+    )(left_image, right_image)
 
 
 def layer(source, weight, span, out_rows, rectify, inside):
@@ -239,8 +243,8 @@
     vreg = (SUBS, NDISP)
     sub = lax.broadcasted_iota(jnp.int32, vreg, 0)
     lane = lax.broadcasted_iota(jnp.int32, vreg, 1)
-    first_edge = jnp.where(sub == 0, BIG_VALUE, 0.0)
-    last_edge = jnp.where(sub == SUBS - 1, BIG_VALUE, 0.0)
+    first_edge = jnp.where(sub == 0, BIG_VALUE, PENALTY_SMALL)
+    last_edge = jnp.where(sub == SUBS - 1, BIG_VALUE, PENALTY_SMALL)
     near_row = lax.broadcasted_iota(jnp.int32, (NDISP, NDISP), 0)
     near_col = lax.broadcasted_iota(jnp.int32, (NDISP, NDISP), 1)
     order = ((near_row % SUBS) * LEADS + near_row // SUBS == near_col).astype(jnp.float32)
@@ -279,19 +283,19 @@
         while len(lowest) > 1:
             lowest = [jnp.minimum(lowest[i], lowest[i + 1]) for i in range(0, len(lowest), 2)]
         lowest = lowest[0]
-        for shift in (4, 2, 1):
-            lowest = jnp.minimum(lowest, pltpu.roll(lowest, shift, 0))
-        below = jnp.maximum(pltpu.roll(state[LEADS - 1], 1, 0), first_edge)
-        above = jnp.maximum(pltpu.roll(state[0], SUBS - 1, 0), last_edge)
-        ext = [below, *state, above]
+        lowest = jnp.minimum(lowest, pltpu.roll(lowest, 4, 0))
+        turned = [pltpu.roll(lowest, shift, 0) for shift in (1, 2, 3)]
+        lowest = jnp.minimum(
+            jnp.minimum(lowest, turned[0]), jnp.minimum(turned[1], turned[2])
+        )
+        jump = lowest + PENALTY_LARGE
+        below = pltpu.roll(state[LEADS - 1], 1, 0) + first_edge
+        above = pltpu.roll(state[0], SUBS - 1, 0) + last_edge
+        ext = [below, *(value + PENALTY_SMALL for value in state), above]
         new = []
         for lead in range(LEADS):
-            near = jnp.minimum(
-                state[lead], jnp.minimum(ext[lead], ext[lead + 2]) + PENALTY_SMALL
-            )
-            new.append(
-                jnp.minimum(near + here[lead], lowest + (here[lead] + PENALTY_LARGE))
-            )
+            near = jnp.minimum(state[lead], jnp.minimum(ext[lead], ext[lead + 2]))
+            new.append(jnp.minimum(near, jump) + here[lead])
         return tuple(new), lowest
 
     def run(axis, place, size, backward, send, recv, send_sem, recv_sem, sweep):
@@ -337,7 +341,7 @@
             return state, lowest
 
         state, lowest = lax.fori_loop(
-            0, tile_cols, body, (state, jnp.zeros(vreg, jnp.float32)), unroll=2
+            0, tile_cols, body, (state, jnp.zeros(vreg, jnp.float32)), unroll=8
         )
         packed = state[0] - lowest
         for lead in range(1, LEADS):
@@ -478,7 +482,7 @@
     weights = (first_weight, second_weight, third_weight)
     tile_rows, tile_cols = left_image.shape
     rows, cols = lax.axis_size("row"), lax.axis_size("col")
-    blocks = exchange(jnp.stack([left_image, right_image]).astype(jnp.float32))
+    blocks = exchange(left_image, right_image)
     place = jnp.stack(
         [
             tile_base[0, 0],

time: 70.5 us -> 65.8 us (0.933)
  Pallas kernels: 65.7 us -> 62.4 us
  local copies, waits for them, and re-layouts: 2.55 us -> 1.78 us
    pallas_call x1, Pallas kernels: 52.9 us -> 49.6 us  [aggregate(): pl.pallas_call(partial(path_kernel, tile_rows, tile_cols), out_shape=jax....]
    unnamed x14 -> x10, local copies, waits for them, and re-layouts: 2.47 us -> 1.7 us
where the time goes in v4:
time: 65.8 us; the launch traced here: 65.6 us
  Pallas kernels  62.4 us (95%)
  local copies, waits for them, and re-layouts  1.78 us (3%)
  between operations  1.37 us (2%)
    pallas_call x1, Pallas kernels, aggregate(): pl.pallas_call(partial(path_kernel, tile_rows, tile_cols), out_shape=jax....  49.6 us
    pallas_call x1, Pallas kernels, exchange(): pl.pallas_call(exchange_kernel, out_shape=jax.ShapeDtypeStruct((ROW_BLOCK...  8.13 us
    pallas_call x1, Pallas kernels, cost_volume(): pl.pallas_call(partial(cost_kernel, tile_rows, tile_cols), out_shape=jax....  4.68 us
    unnamed x10, local copies, waits for them, and re-layouts  1.7 us

profile of v4, /device:TPU:0, one launch (start us, length us, event | category | flops | bytes accessed | tf_op | source)
XLA Modules:
  0.0 65.6 jit_solution(13633644124120747903)
XLA Ops:
  0.7 0.0 copy-start.3
  1.3 0.1 stack.11.place_ref
  1.4 0.0 copy-done.3
  1.4 0.1 copy.8.first_ref
  1.5 0.0 copy-start.1
  1.5 0.0 copy-start.2
  1.5 8.1 %exchange.1.blocks_ref = f32[3,4,2,8,128]{4,3,2,1,0:T(8,128)} custom-call(bf16[8,128]{1,0:T(8,128)(2,1)} %left_ref.1, bf16[8,128]{1,0:T(8,128)(2,1)} %right_ref.1), custom_call_target="tpu_custom_call" | custom-call | tf_op jit(solution)/shard_map/exchange/pallas_call | solution.py:92
  9.7 0.0 copy-done.1
  9.7 0.0 copy-done.2
  9.7 0.0 copy-start
  9.7 0.9 %copy-done = f32[3,4,2,8,128]{4,3,2,1,0:T(8,128)S(1)} copy-done((f32[3,4,2,8,128]{4,3,2,1,0:T(8,128)S(1)}, f32[3,4,2,8,128]{4,3,2,1,0:T(8,128)}, u32[]{:S(2)}) %copy-start) | copy-done | bytes 98328
  10.6 4.7 %costs.1.volume_ref = bf16[8,128,128]{2,1,0:T(8,128)(2,1)S(1)} custom-call(s32[6]{0:T(128)S(1)} %stack.11.place_ref, f32[3,4,2,8,128]{4,3,2,1,0:T(8,128)S(1)} %copy-done, bf16[32,9]{1,0:T(8,128)(2,1)S(1)} %copy.8.first_ref, bf16[32,288]{1,0:T(8,128)(2,1)S(1)} %copy-done.1, bf16[32,288]{1,0:T(8,128)(2,1)S(1)} %copy-done.2), custom_call_target="tpu_custom_call" | custom-call | tf_op jit(solution)/shard_map/costs/pallas_call | solution.py:187
  15.2 49.6 %paths.1 = bf16[8,128,128]{2,1,0:T(8,128)(2,1)S(1)} custom-call(bf16[8,128,128]{2,1,0:T(8,128)(2,1)S(1)} %costs.1.volume_ref), custom_call_target="tpu_custom_call" | custom-call | tf_op jit(solution)/shard_map/paths/pallas_call | solution.py:452
  64.9 0.7 %copy.12 = bf16[8,128,128]{2,1,0:T(8,128)(2,1)} copy(bf16[8,128,128]{2,1,0:T(8,128)(2,1)S(1)} %paths.1) | data formatting | bytes 524288
Async XLA Ops:
  0.7 0.8 %copy-start.3 = (bf16[32,9]{0,1:T(8,128)(2,1)S(1)}, bf16[32,9]{0,1:T(8,128)(2,1)}, u32[]{:S(2)}) copy-start(bf16[32,9]{0,1:T(8,128)(2,1)} %param.9) | copy-start | bytes 1732
  1.5 8.1 %copy-start.1 = (bf16[32,288]{1,0:T(8,128)(2,1)S(1)}, bf16[32,288]{1,0:T(8,128)(2,1)}, u32[]{:S(2)}) copy-start(bf16[32,288]{1,0:T(8,128)(2,1)} %second_ref.1) | copy-start | bytes 55300
  1.5 8.2 %copy-start.2 = (bf16[32,288]{1,0:T(8,128)(2,1)S(1)}, bf16[32,288]{1,0:T(8,128)(2,1)}, u32[]{:S(2)}) copy-start(bf16[32,288]{1,0:T(8,128)(2,1)} %third_ref.1) | copy-start | bytes 55300
  9.7 0.9 %copy-start = (f32[3,4,2,8,128]{4,3,2,1,0:T(8,128)S(1)}, f32[3,4,2,8,128]{4,3,2,1,0:T(8,128)}, u32[]{:S(2)}) copy-start(f32[3,4,2,8,128]{4,3,2,1,0:T(8,128)} %exchange.1.blocks_ref) | copy-start | bytes 294916

commit v5 on v4

--- a/solution.py
+++ b/solution.py
@@ -404,7 +404,7 @@
 
         lax.fori_loop(0, tile_rows, gather_row, 0)
 
-    late = 2 * jnp.minimum(col, cols - 1 - col) >= cols // 2
+    late = 2 * jnp.minimum(col, cols - 1 - col) > cols // 2
 
     @pl.when(late)
     def _():

time: 65.8 us -> 65.8 us (level)
  no operation moved by 1% of the time
where the time goes in v5:
time: 65.8 us; the launch traced here: 65.6 us
  Pallas kernels  62.4 us (95%)
  local copies, waits for them, and re-layouts  1.78 us (3%)
  between operations  1.37 us (2%)
    pallas_call x1, Pallas kernels, aggregate(): pl.pallas_call(partial(path_kernel, tile_rows, tile_cols), out_shape=jax....  49.6 us
    pallas_call x1, Pallas kernels, exchange(): pl.pallas_call(exchange_kernel, out_shape=jax.ShapeDtypeStruct((ROW_BLOCK...  8.13 us
    pallas_call x1, Pallas kernels, cost_volume(): pl.pallas_call(partial(cost_kernel, tile_rows, tile_cols), out_shape=jax....  4.68 us
    unnamed x10, local copies, waits for them, and re-layouts  1.7 us

profile of v5, /device:TPU:0, one launch (start us, length us, event | category | flops | bytes accessed | tf_op | source)
XLA Modules:
  0.0 65.6 jit_solution(15745200092960025596)
XLA Ops:
  0.7 0.0 copy-start.3
  1.3 0.1 stack.11.place_ref
  1.4 0.0 copy-done.3
  1.4 0.1 copy.8.first_ref
  1.5 0.0 copy-start.1
  1.5 0.0 copy-start.2
  1.5 8.1 %exchange.1.blocks_ref = f32[3,4,2,8,128]{4,3,2,1,0:T(8,128)} custom-call(bf16[8,128]{1,0:T(8,128)(2,1)} %left_ref.1, bf16[8,128]{1,0:T(8,128)(2,1)} %right_ref.1), custom_call_target="tpu_custom_call" | custom-call | tf_op jit(solution)/shard_map/exchange/pallas_call | solution.py:92
  9.7 0.0 copy-done.1
  9.7 0.0 copy-done.2
  9.7 0.0 copy-start
  9.7 0.9 %copy-done = f32[3,4,2,8,128]{4,3,2,1,0:T(8,128)S(1)} copy-done((f32[3,4,2,8,128]{4,3,2,1,0:T(8,128)S(1)}, f32[3,4,2,8,128]{4,3,2,1,0:T(8,128)}, u32[]{:S(2)}) %copy-start) | copy-done | bytes 98328
  10.6 4.7 %costs.1.volume_ref = bf16[8,128,128]{2,1,0:T(8,128)(2,1)S(1)} custom-call(s32[6]{0:T(128)S(1)} %stack.11.place_ref, f32[3,4,2,8,128]{4,3,2,1,0:T(8,128)S(1)} %copy-done, bf16[32,9]{1,0:T(8,128)(2,1)S(1)} %copy.8.first_ref, bf16[32,288]{1,0:T(8,128)(2,1)S(1)} %copy-done.1, bf16[32,288]{1,0:T(8,128)(2,1)S(1)} %copy-done.2), custom_call_target="tpu_custom_call" | custom-call | tf_op jit(solution)/shard_map/costs/pallas_call | solution.py:187
  15.2 49.6 %paths.1 = bf16[8,128,128]{2,1,0:T(8,128)(2,1)S(1)} custom-call(bf16[8,128,128]{2,1,0:T(8,128)(2,1)S(1)} %costs.1.volume_ref), custom_call_target="tpu_custom_call" | custom-call | tf_op jit(solution)/shard_map/paths/pallas_call | solution.py:452
  64.9 0.7 %copy.12 = bf16[8,128,128]{2,1,0:T(8,128)(2,1)} copy(bf16[8,128,128]{2,1,0:T(8,128)(2,1)S(1)} %paths.1) | data formatting | bytes 524288
Async XLA Ops:
  0.7 0.8 %copy-start.3 = (bf16[32,9]{0,1:T(8,128)(2,1)S(1)}, bf16[32,9]{0,1:T(8,128)(2,1)}, u32[]{:S(2)}) copy-start(bf16[32,9]{0,1:T(8,128)(2,1)} %param.9) | copy-start | bytes 1732
  1.5 8.1 %copy-start.1 = (bf16[32,288]{1,0:T(8,128)(2,1)S(1)}, bf16[32,288]{1,0:T(8,128)(2,1)}, u32[]{:S(2)}) copy-start(bf16[32,288]{1,0:T(8,128)(2,1)} %second_ref.1) | copy-start | bytes 55300
  1.5 8.2 %copy-start.2 = (bf16[32,288]{1,0:T(8,128)(2,1)S(1)}, bf16[32,288]{1,0:T(8,128)(2,1)}, u32[]{:S(2)}) copy-start(bf16[32,288]{1,0:T(8,128)(2,1)} %third_ref.1) | copy-start | bytes 55300
  9.7 0.9 %copy-start = (f32[3,4,2,8,128]{4,3,2,1,0:T(8,128)S(1)}, f32[3,4,2,8,128]{4,3,2,1,0:T(8,128)}, u32[]{:S(2)}) copy-start(f32[3,4,2,8,128]{4,3,2,1,0:T(8,128)} %exchange.1.blocks_ref) | copy-start | bytes 294916
